TPU v7x, 128 devices: a whole 4x4x4 slice. The times are simulated.
128 devices in a mesh: tm: 16 (over y, x_hi, core), unit: 8 (over x_lo, z).
Axes of the slice: x: 4 (x_hi: 2, x_lo: 2; x = x_hi * 2 + x_lo), y: 4, z: 4, core: 2. Of those that a mesh axis runs over, the one named last changes fastest.
Arguments:
- recording: bfloat16 [131072, 384], P(('tm', 'unit')), may hold values from -6 to 6
- spike_times: int32 [4096], P(('tm', 'unit')), may hold values from 30 to 131041, as said below
- unit_labels: int32 [4096], P(('tm', 'unit')), may hold values from 0 to 511, as said below
- old_templates: bfloat16 [512, 23424], P('unit'), may hold values from -3 to 3
Outputs:
- templates: bfloat16 [512, 23424], P('unit', 'tm')
- scores: float32 [512, 65536], P('unit', 'tm')
Inputs may be any that keep to these rules, and one draw needn't show every extreme that they name: `spike_times`: the spikes lie in blocks of 32, block b on the device of flattened index b over tm and unit; the times of block b lie in b * 1024 + 30 to (b + 1) * 1024 - 31, and both ends are reached in every block. `unit_labels`: labels lie in 0 to 511; the panel of a label is label // 64. In each block of 32 spikes at most 8 labels fall in one panel, and on each index of tm one panel receives exactly 8 from every block of that index.
All inputs are finite; a program needn't handle non-finite values.
Results may differ from a plain program's by a relative error of at most 0.0027.
Values may be sent and summed in bfloat16 or wider, within the bound.
A program may use at most 64 MiB of HBM per device.

v0:
```python
import jax
import jax.numpy as jnp
from jax import lax
from jax.sharding import PartitionSpec as P

STRIDE = 2
CAP = 8


def from_behind(value, axis, by):
    size = lax.axis_size(axis)
    pairs = [(i, i + by) for i in range(size) if 0 <= i + by < size]
    return lax.ppermute(value, axis, pairs)


def refine(sums, counts, old):
    weight = counts / (counts + 4.0)
    mean = sums / jnp.maximum(counts, 1.0)[:, None]
    base = old.astype(jnp.float32)
    return (base + weight[:, None] * (mean - base)).astype(jnp.bfloat16)


def correlate(extended, kernel_rows, channels, taps):
    kernel = kernel_rows.reshape(kernel_rows.shape[0], channels, taps)
    out = lax.conv_general_dilated(
        extended[None],
        kernel,
        (STRIDE,),
        "VALID",
        dimension_numbers=("NWC", "OIW", "NCW"),
        preferred_element_type=jnp.float32,
    )
    return out[0]


def body(recording, spike_times, unit_labels, old_templates):
    sub_rows, chans = recording.shape
    panel, feat = old_templates.shape
    taps = feat // chans
    half = (taps - 1) // 2
    owners = lax.axis_size("unit")
    tm_count = lax.axis_size("tm")
    spikes = spike_times.shape[0]
    tm_pos = lax.axis_index("tm")
    unit_pos = lax.axis_index("unit")
    scale = 1.0 / jnp.sqrt(jnp.float32(feat))
    flat_pos = tm_pos * owners + unit_pos
    local = spike_times - flat_pos * sub_rows - half
    snips = jax.vmap(lambda s: lax.dynamic_slice(recording, (s, jnp.int32(0)), (taps, chans)))(
        local
    )
    snippet_rows = jnp.transpose(snips, (0, 2, 1)).reshape(spikes, feat)
    owner = unit_labels // panel
    within = unit_labels % panel
    owner_hits = (owner[:, None] == jnp.arange(owners)[None, :]).astype(jnp.int32)
    earlier = jnp.cumsum(owner_hits, axis=0) - owner_hits
    rank = jnp.sum(earlier * owner_hits, axis=1)
    target = owner * CAP + rank
    placing = jnp.arange(owners * CAP)[:, None] == target[None, :]
    send_rows = jnp.dot(
        placing.astype(jnp.bfloat16), snippet_rows, preferred_element_type=jnp.float32
    )
    send_rows = send_rows.astype(jnp.bfloat16).reshape(owners, CAP, feat)
    send_tags = jnp.dot(placing.astype(jnp.float32), within.astype(jnp.float32) + 1.0) - 1.0
    send_tags = send_tags.astype(jnp.bfloat16).reshape(owners, CAP)
    got_rows, got_tags = (
        lax.all_to_all(send_rows, "unit", split_axis=0, concat_axis=0, tiled=True),
        lax.all_to_all(send_tags, "unit", split_axis=0, concat_axis=0, tiled=True),
    )
    matching = (
        got_tags.astype(jnp.float32).reshape(1, -1) == jnp.arange(panel, dtype=jnp.float32)[:, None]
    )
    sums = jnp.dot(
        matching.astype(jnp.bfloat16),
        got_rows.reshape(-1, feat),
        preferred_element_type=jnp.float32,
    )
    counts = jnp.sum(matching.astype(jnp.float32), axis=1)
    whole_slab = lax.all_gather(recording, "unit", axis=0, tiled=True)
    following = from_behind(whole_slab[: taps - 1], "tm", -1)
    extended = jnp.concatenate([whole_slab, following], axis=0)
    share = feat // tm_count
    total_sums, total_counts = lax.psum((sums, counts), "tm")
    refined = refine(total_sums, total_counts, old_templates)
    raw_scores = correlate(extended, refined, chans, taps)
    out_templates = lax.dynamic_slice_in_dim(refined, tm_pos * share, share, 1)
    return (out_templates, raw_scores * scale)


def solution(mesh):
    in_specs = (P(("tm", "unit"), None), P(("tm", "unit")), P(("tm", "unit")), P("unit", None))
    out_specs = (P("unit", "tm"), P("unit", "tm"))
    return jax.shard_map(body, mesh=mesh, in_specs=in_specs, out_specs=out_specs, check_vma=False)
```

profile of v0, /device:TPU:1, one launch (start us, length us, event | category | flops | bytes accessed | tf_op | source)
XLA Modules:
  0.0 506.5 jit_solution(7749047966560364088)
XLA Ops:
  8.0 0.7 and_select_fusion.1
  9.0 0.7 multiply_add_fusion
  9.6 0.8 fusion.15
  10.4 0.7 all_to_all.12
  11.1 6.8 %all-to-all-start = ((bf16[8,1,8]{2,1,0:T(2,128)(2,1)}), bf16[8,1,8]{2,1,0:T(2,128)(2,1)S(1)}, u32[]{:S(2)}, u32[]{:S(2)}) async-start(bf16[8,1,8]{2,1,0:T(2,128)(2,1)} %all_to_all.12), calls=%async_computation | async-start | bytes 8192 | tf_op jit(solution)/shard_map/all_to_all | solution.py:68
  17.9 0.7 fusion.24
  18.6 85.5 %while.1 = (s32[]{:T(128)}, bf16[1024,384]{1,0:T(8,128)(2,1)}, s32[32,2]{0,1:T(2,128)S(1)}, bf16[32,61,384]{2,1,0:T(8,128)(2,1)}, s32[]{:T(128)}) while((s32[]{:T(128)}, bf16[1024,384]{1,0:T(8,128)(2,1)}, s32[32,2]{0,1:T(2,128)S(1)}, bf16[32,61,384]{2,1,0:T(8,128)(2,1)}, s32[]{:T(128)}) %tuple.21), condition=%wide.while_cond, body=%wide.while_body.sunk | while | flops 2 | bytes 99417 | solution.py:49
  19.2 2.0 bitcast_dynamic-update-slice_fusion.2
  21.9 2.1 bitcast_dynamic-update-slice_fusion.2
  24.5 2.1 bitcast_dynamic-update-slice_fusion.2
  26.7 0.5 slice.22
  27.2 2.1 bitcast_dynamic-update-slice_fusion.2
  29.9 2.1 bitcast_dynamic-update-slice_fusion.2
  32.5 2.1 bitcast_dynamic-update-slice_fusion.2
  35.2 2.1 bitcast_dynamic-update-slice_fusion.2
  37.3 0.5 slice.22
  37.9 2.0 bitcast_dynamic-update-slice_fusion.2
  40.5 2.1 bitcast_dynamic-update-slice_fusion.2
  43.2 2.1 bitcast_dynamic-update-slice_fusion.2
  45.9 2.0 bitcast_dynamic-update-slice_fusion.2
  48.5 2.1 bitcast_dynamic-update-slice_fusion.2
  51.2 2.1 bitcast_dynamic-update-slice_fusion.2
  53.4 0.5 slice.22
  53.9 2.1 bitcast_dynamic-update-slice_fusion.2
  56.0 0.5 slice.22
  56.6 2.1 bitcast_dynamic-update-slice_fusion.2
  59.2 2.1 bitcast_dynamic-update-slice_fusion.2
  61.9 2.1 bitcast_dynamic-update-slice_fusion.2
  64.6 2.1 bitcast_dynamic-update-slice_fusion.2
  67.2 2.1 bitcast_dynamic-update-slice_fusion.2
  69.9 2.1 bitcast_dynamic-update-slice_fusion.2
  72.6 2.1 bitcast_dynamic-update-slice_fusion.2
  75.3 2.0 bitcast_dynamic-update-slice_fusion.2
  77.9 2.1 bitcast_dynamic-update-slice_fusion.2
  80.6 2.0 bitcast_dynamic-update-slice_fusion.2
  83.3 2.1 bitcast_dynamic-update-slice_fusion.2
  86.0 2.1 bitcast_dynamic-update-slice_fusion.2
  88.6 2.1 bitcast_dynamic-update-slice_fusion.2
  91.3 2.0 bitcast_dynamic-update-slice_fusion.2
  94.0 2.1 bitcast_dynamic-update-slice_fusion.2
  96.6 2.0 bitcast_dynamic-update-slice_fusion.2
  99.3 2.1 bitcast_dynamic-update-slice_fusion.2
  102.0 2.1 bitcast_dynamic-update-slice_fusion.2
  104.0 3.1 copy.25
  107.1 5.5 %reshape.34 = bf16[32,23424]{1,0:T(8,128)(2,1)} reshape(bf16[32,384,61]{2,1,0:T(8,128)(2,1)S(1)} %copy.25) | data formatting | bytes 2998272 | tf_op jit(solution)/shard_map/reshape | solution.py:52
  112.6 3.9 fusion
  116.5 5.1 %all-to-all-start.1 = ((bf16[8,8,23424]{2,1,0:T(8,128)(2,1)}), bf16[8,8,23424]{2,1,0:T(8,128)(2,1)S(1)}, u32[]{:S(2)}, u32[]{:S(2)}) async-start(bf16[8,8,23424]{2,1,0:T(8,128)(2,1)} %fusion), calls=%async_computation.1 | async-start | bytes 5996544 | tf_op jit(solution)/shard_map/all_to_all | solution.py:67
  121.8 35.6 %all-to-all-done.1 = bf16[8,8,23424]{2,1,0:T(8,128)(2,1)S(1)} async-done(((bf16[8,8,23424]{2,1,0:T(8,128)(2,1)}), bf16[8,8,23424]{2,1,0:T(8,128)(2,1)S(1)}, u32[]{:S(2)}, u32[]{:S(2)}) %all-to-all-start.1) | async-done | bytes 2998304 | tf_op jit(solution)/shard_map/all_to_all | solution.py:67
  157.5 3.5 fusion.12
  161.7 33.7 %psum.14 = f32[64]{0:T(128)S(1)} all-reduce(f32[64]{0:T(128)S(1)} %convert_reduce_fusion), channel_id=1, replica_groups=mesh['tm'=16,'unit'=8] {'tm'}, use_global_device_ids=true, to_apply=%region_3.4 | all-reduce | flops 64 | bytes 512 | tf_op jit(solution)/shard_map/psum | solution.py:83
  195.4 185.1 %all-reduce.3.cloned.1.call-done = f32[64,23424]{1,0:T(8,128)} async-done(((f32[64,23424]{1,0:T(8,128)}), f32[64,23424]{1,0:T(8,128)}) %all-reduce.3.cloned.1.call-update) | async-done | bytes 5996560 | tf_op jit(solution)/shard_map/psum | solution.py:83
  380.5 4.8 fusion.10
  385.3 0.8 slice.17
  386.1 5.1 %collective-permute-start = (bf16[60,384]{1,0:T(8,128)(2,1)S(1)}, bf16[60,384]{1,0:T(8,128)(2,1)S(1)}, u32[]{:S(2)}, u32[]{:S(2)}) collective-permute-start(bf16[60,384]{1,0:T(8,128)(2,1)S(1)} %slice.17), channel_id=1, source_target_pairs={{8,0},{16,8},{24,16},{32,24},{40,32},{48,40},{56,48},{64,56},{72,6... | collective-permute-start | bytes 138248 | tf_op jit(solution)/shard_map/ppermute | solution.py:13
  391.2 0.8 constant_dynamic-slice_fusion.1
  392.0 19.6 %reshape.37 = bf16[64,384,61]{2,1,0:T(8,128)(2,1)} reshape(bf16[64,23424]{1,0:T(8,128)(2,1)S(1)} %fusion.10) | data formatting | bytes 5996544 | tf_op jit(solution)/shard_map/reshape | solution.py:24
  411.6 7.3 %copy.28 = bf16[64,384,61]{1,0,2:T(8,128)(2,1)S(1)} copy(bf16[64,384,61]{2,1,0:T(8,128)(2,1)} %reshape.37) | data formatting | bytes 5996544 | tf_op jit(solution)/shard_map/reshape | solution.py:24
  418.9 10.1 %maximum_bitcast_fusion = bf16[1,8252,384]{2,1,0:T(8,128)(2,1)S(1)} fusion(bf16[60,384]{1,0:T(8,128)(2,1)S(1)} %collective-permute-done, bf16[8192,384]{1,0:T(8,128)(2,1)} %all-gather.2.cloned.1.call-done), kind=kLoop, calls=%fused_computation.14 | loop fusion | flops 12675072 | bytes 12675072 | tf_op jit(solution)/shard_map/broadcast_in_dim | solution.py:26
  429.0 2.6 pad.3
  431.6 5.9 %copy.27 = bf16[1,8,1032,384]{3,1,2,0:T(8,128)(2,1)S(1)} copy(bf16[1,8,1032,384]{3,2,1,0:T(8,128)(2,1)S(1)} %bitcast.41) | data formatting | bytes 12681216 | tf_op jit(solution)/shard_map/conv_general_dilated | solution.py:25
  437.6 56.5 %fusion.4 = f32[8,516,64]{2,0,1:T(8,128)} fusion(bf16[64,384,61]{1,0,2:T(8,128)(2,1)S(1)} %copy.28, bf16[1,7,60,384]{3,1,2,0:T(8,128)(2,1)S(1)} %slice.18, bf16[1,8,1032,384]{3,1,2,0:T(8,128)(2,1)S(1)} %copy.27), kind=kOutput, calls=%fused_computation.10 | convolution fusion | flops 12396994560 | bytes 10718208 | tf_op jit(solution)/shard_map/conv_general_dilated | solution.py:25
  494.2 2.5 copy.29
  496.8 0.8 copy.30
  498.0 1.0 slice_bitcast_fusion
  (81 shorter events, 19.3 us)
Async XLA Ops:
  11.1 105.4 %all-to-all-start = ((bf16[8,1,8]{2,1,0:T(2,128)(2,1)}), bf16[8,1,8]{2,1,0:T(2,128)(2,1)S(1)}, u32[]{:S(2)}, u32[]{:S(2)}) async-start(bf16[8,1,8]{2,1,0:T(2,128)(2,1)} %all_to_all.12), calls=%async_computation | async-start | bytes 8192 | tf_op jit(solution)/shard_map/all_to_all | solution.py:68
  116.5 40.9 %all-to-all-start.1 = ((bf16[8,8,23424]{2,1,0:T(8,128)(2,1)}), bf16[8,8,23424]{2,1,0:T(8,128)(2,1)S(1)}, u32[]{:S(2)}, u32[]{:S(2)}) async-start(bf16[8,8,23424]{2,1,0:T(8,128)(2,1)} %fusion), calls=%async_computation.1 | async-start | bytes 5996544 | tf_op jit(solution)/shard_map/all_to_all | solution.py:67
  121.7 258.8 %all-reduce.3.cloned.1.call-start = ((), (), s32[]{:S(2)}) async-start(), calls=%async_computation.2 | async-start | bytes 11993088 | tf_op jit(solution)/shard_map/psum | solution.py:83
  161.0 224.3 %all-gather.2.cloned.1.call-start = ((), (), s32[]{:S(2)}) async-start(), calls=%async_computation.3 | async-start | bytes 7077888 | tf_op jit(solution)/shard_map/all_gather | solution.py:79
  386.1 32.8 %collective-permute-start = (bf16[60,384]{1,0:T(8,128)(2,1)S(1)}, bf16[60,384]{1,0:T(8,128)(2,1)S(1)}, u32[]{:S(2)}, u32[]{:S(2)}) collective-permute-start(bf16[60,384]{1,0:T(8,128)(2,1)S(1)} %slice.17), channel_id=1, source_target_pairs={{8,0},{16,8},{24,16},{32,24},{40,32},{48,40},{56,48},{64,56},{72,6... | collective-permute-start | bytes 138248 | tf_op jit(solution)/shard_map/ppermute | solution.py:13
  494.2 2.5 copy-start
Sparse Core Ops, SparseCore 0:
  161.1 219.3 all-reduce.2
Sparse Core Ops, SparseCore 1:
  163.2 97.9 all-gather.1
where the time goes:
time: 509 us; the launch traced here: 506 us
  waiting for transfers between devices  221 us (43%)
  local copies, waits for them, and re-layouts  136 us (27%)
  matrix products  64.7 us (13%)
  blocking collectives  33.7 us (7%)
  other arithmetic  17.5 us (3%)
  starting transfers between devices  17.2 us (3%)
  between operations  15.6 us (3%)
    psum x1, waiting for transfers between devices, body(): total_sums, total_counts = lax.psum((sums, counts), 'tm')  185 us
    gather x96, local copies, waits for them, and re-layouts  85.4 us
    conv_general_dilated x1, matrix products, correlate(): lax.conv_general_dilated(extended[None], kernel, (STRIDE,), 'VALID', dime...  56.5 us
    all_to_all x1, waiting for transfers between devices, body(): lax.all_to_all(send_rows, 'unit', split_axis=0, concat_axis=0, tiled=True)  35.6 us
    psum x1, blocking collectives, body(): total_sums, total_counts = lax.psum((sums, counts), 'tm')  33.7 us
    reshape x2, local copies, waits for them, and re-layouts, correlate(): kernel = kernel_rows.reshape(kernel_rows.shape[0], channels, taps)  26.9 us
  transfers between devices with their start and end apart: 5, of which 2 were waited for; matrix products, arithmetic and copies ran while one was open for 26% of the time, Pallas kernels for 0%

commit v1 on v0

v1 whole, which is shorter than its diff:
```python
import functools

import jax
import jax.numpy as jnp
from jax import lax
from jax.experimental import pallas as pl
from jax.experimental.pallas import tpu as pltpu
from jax.sharding import PartitionSpec as P

MESH = pl.DeviceIdType.MESH
TAPS = 61
CAP = 8
GROUPS = 4
STEP = 16
PHASES = 8
LINES = 128
ROWS = 1056
TAIL = 16
CHUNKS = 3
WIDE = 128
FLAT = STEP + 1


def dot_f32(a, b):
    return jnp.dot(a, b, preferred_element_type=jnp.float32)


def dot_nt(a, b):
    return lax.dot_general(a, b, (((1,), (1,)), ((), ())), preferred_element_type=jnp.float32)


def exchange_kernel(
    own_ref,
    tab_ref,
    old_ref,
    x_ref,
    t_ref,
    v_ref,
    tabs,
    picks,
    snip,
    sums,
    away,
    swap_in,
    part,
    part_in,
    tab_s,
    tab_r,
    ag_s,
    ag_r,
    halo_s,
    halo_r,
    swap_s,
    swap_r,
    rs_s,
    rs_r,
    tg_s,
    tg_r,
    fw_s,
    fw_r,
):
    t = lax.axis_index("tm")
    u = lax.axis_index("unit")
    core = lax.rem(t, 2)
    chip = t // 2
    z = lax.rem(u, 4)
    side = u - z
    other = 4 - side
    zp = lax.rem(z + 1, 4)
    zm = lax.rem(z + 3, 4)
    zo = lax.rem(z + 2, 4)
    up, down, across = side + zp, side + zm, other + z

    barrier = pltpu.get_barrier_semaphore()
    for rel in range(1, 8):
        pl.semaphore_signal(
            barrier, inc=1, device_id={"unit": lax.rem(u + rel, 8)}, device_id_type=MESH
        )
    for rel in range(1, 16):
        pl.semaphore_signal(
            barrier, inc=1, device_id={"tm": lax.rem(t + rel, 16)}, device_id_type=MESH
        )
    pl.semaphore_wait(barrier, 22)

    tab_cp = []
    for rel in range(1, 8):
        to = lax.rem(u + rel, 8)
        c = pltpu.make_async_remote_copy(
            src_ref=tab_ref.at[to],
            dst_ref=tabs.at[u],
            send_sem=tab_s.at[rel - 1],
            recv_sem=tab_r.at[rel - 1],
            device_id={"unit": to},
            device_id_type=MESH,
        )
        c.start()
        tab_cp.append(c)

    row = lax.broadcasted_iota(jnp.int32, (LINES, 1024), 0) * PHASES
    col = lax.broadcasted_iota(jnp.int32, (LINES, 1024), 1)
    mine = pl.ds(pl.multiple_of(u * LINES, LINES), LINES)
    own = own_ref[...]
    for p in range(PHASES):
        pick = jnp.where(col == row + p, 1.0, 0.0).astype(jnp.bfloat16)
        got = dot_f32(pick, own).astype(jnp.bfloat16)
        for cc in range(CHUNKS):
            lane = (cc * PHASES + p) * WIDE
            x_ref[mine, lane : lane + WIDE] = got[:, cc * WIDE : (cc + 1) * WIDE]

    def block(index, cc, first=0, count=LINES):
        return x_ref.at[
            pl.ds(pl.multiple_of(index * LINES + first, 16), count),
            cc * PHASES * WIDE : (cc + 1) * PHASES * WIDE,
        ]

    def hop(cc, k, ref, to):
        return pltpu.make_async_remote_copy(
            src_ref=ref,
            dst_ref=ref,
            send_sem=ag_s.at[cc * 8 + k],
            recv_sem=ag_r.at[cc * 8 + k],
            device_id={"unit": to},
            device_id_type=MESH,
        )

    half = LINES // 2
    hops = []
    for cc in range(CHUNKS):
        hops.append(
            [
                hop(cc, 0, block(u, cc), across),
                hop(cc, 1, block(u, cc), up),
                hop(cc, 2, block(u, cc), down),
                hop(cc, 3, block(down, cc, 0, half), up),
                hop(cc, 4, block(up, cc, half, half), down),
                hop(cc, 5, block(across, cc), up),
                hop(cc, 6, block(across, cc), down),
                hop(cc, 7, block(side + zo, cc), across),
            ]
        )

    def own_sends(cc):
        for k in (0, 1, 2):
            hops[cc][k].start()

    def forward_one(cc):
        hops[cc][0].wait_recv()
        hops[cc][5].start()
        hops[cc][6].start()
        hops[cc][1].wait_recv()
        hops[cc][3].start()
        hops[cc][2].wait_recv()
        hops[cc][4].start()

    def forward_two(cc):
        hops[cc][3].wait_recv()
        hops[cc][4].wait_recv()
        hops[cc][7].start()

    def finish(cc):
        hops[cc][5].wait_recv()
        hops[cc][6].wait_recv()
        hops[cc][7].wait_recv()

    own_sends(0)

    tabs[u] = tab_ref[u]
    for c in tab_cp:
        c.wait_recv()

    tval = lax.broadcasted_iota(jnp.int32, (CAP, 1024), 1)
    tval = (tval % LINES) * PHASES + tval // LINES
    lead = lax.broadcasted_iota(jnp.int32, (GROUPS * STEP, 1, 1), 0)
    tap = (lead % GROUPS) * STEP + lead // GROUPS
    tap = jnp.where(tap < TAPS, tap, -100000)
    order = [u, across, up, down, side + zo, other + zp, other + zm, other + zo]

    def build_picks(i, carry):
        start = tabs[i][:, 0:1]
        gap = (tval - start)[None]
        pick = jnp.where(gap == tap, 1.0, 0.0).reshape(GROUPS * STEP * CAP, 1024)
        picks[i] = pick.astype(jnp.bfloat16)
        return carry

    lax.fori_loop(0, 8, build_picks, 0)

    labels = tabs[...].reshape(64, 128)[:, 64:65]
    labels = jnp.concatenate([labels] * GROUPS, axis=0)
    r4 = lax.broadcasted_iota(jnp.int32, (256, 256), 0)
    c4 = lax.broadcasted_iota(jnp.int32, (256, 256), 1)
    merge = jnp.where(
        jnp.logical_and(labels == c4 % 64, r4 // 64 == c4 // 64), 1.0, 0.0
    )
    merge = merge.T.astype(jnp.bfloat16)
    tally = dot_f32(merge, jnp.ones((256, WIDE), jnp.bfloat16))

    def gather(cc, position):
        b = order[position]
        base = cc * PHASES * WIDE
        rows = pl.ds(pl.multiple_of(b * LINES, LINES), LINES)
        data = jnp.concatenate(
            [x_ref[rows, base + p * WIDE : base + (p + 1) * WIDE] for p in range(PHASES)],
            axis=0,
        )
        cut = dot_f32(picks[b], data)
        at = pl.ds(pl.multiple_of(b * CAP, CAP), CAP)
        for j in range(STEP):
            for g in range(GROUPS):
                r = (j * GROUPS + g) * CAP
                snip[g, at, j * WIDE : (j + 1) * WIDE] = cut[r : r + CAP]

    def halo(cc):
        lanes = pl.ds(cc * PHASES * WIDE, PHASES * WIDE)
        return pltpu.make_async_remote_copy(
            src_ref=x_ref.at[pl.ds(0, TAIL), lanes],
            dst_ref=x_ref.at[pl.ds(1024, TAIL), lanes],
            send_sem=halo_s.at[cc],
            recv_sem=halo_r.at[cc],
            device_id={"tm": lax.rem(t + 15, 16)},
            device_id_type=MESH,
        )

    halos = [halo(cc) for cc in range(CHUNKS)]

    def swap(cc):
        return pltpu.make_async_remote_copy(
            src_ref=away.at[cc],
            dst_ref=swap_in.at[cc],
            send_sem=swap_s.at[cc],
            recv_sem=swap_r.at[cc],
            device_id={"tm": chip * 2 + 1 - core},
            device_id_type=MESH,
        )

    swaps = [swap(cc) for cc in range(CHUNKS)]

    def merge_labels(cc):
        out = dot_f32(merge, snip[...].reshape(256, STEP * WIDE).astype(jnp.bfloat16))
        out = jnp.concatenate([out, tally], axis=1).reshape(8, 2, 16, FLAT * WIDE)
        sums[cc] = out
        away[cc] = sums[cc, :, 1 - core].astype(jnp.bfloat16)
        swaps[cc].start()

    def scatter(cc, rel):
        to = lax.rem(chip + rel, 8)
        return pltpu.make_async_remote_copy(
            src_ref=part.at[cc, to],
            dst_ref=part_in.at[cc, rel - 1],
            send_sem=rs_s.at[cc * 7 + rel - 1],
            recv_sem=rs_r.at[cc * 7 + rel - 1],
            device_id={"tm": to * 2 + core},
            device_id_type=MESH,
        )

    scatters = [[scatter(cc, rel) for rel in range(1, 8)] for cc in range(CHUNKS)]

    def reduce_start(cc):
        swaps[cc].wait_recv()
        part[cc] = (sums[cc, :, core] + swap_in[cc].astype(jnp.float32)).astype(jnp.bfloat16)
        for c in scatters[cc]:
            c.start()

    def panel(cc, ch, co):
        return t_ref.at[ch, co, :, cc * STEP * WIDE : (cc + 1) * STEP * WIDE]

    def give(cc, rel):
        return pltpu.make_async_remote_copy(
            src_ref=panel(cc, chip, core),
            dst_ref=panel(cc, chip, core),
            send_sem=tg_s.at[cc * 7 + rel - 1],
            recv_sem=tg_r.at[cc * 7 + rel - 1],
            device_id={"tm": lax.rem(chip + rel, 8) * 2 + core},
            device_id_type=MESH,
        )

    def pass_on(cc, rel):
        ch = lax.rem(chip + 8 - rel, 8)
        return pltpu.make_async_remote_copy(
            src_ref=panel(cc, ch, core),
            dst_ref=panel(cc, ch, core),
            send_sem=fw_s.at[cc * 8 + rel],
            recv_sem=fw_r.at[cc * 8 + rel],
            device_id={"tm": chip * 2 + 1 - core},
            device_id_type=MESH,
        )

    gives = [[give(cc, rel) for rel in range(1, 8)] for cc in range(CHUNKS)]
    passes = [[pass_on(cc, rel) for rel in range(8)] for cc in range(CHUNKS)]

    def refine(cc):
        for c in scatters[cc]:
            c.wait_recv()
        total = sums[cc, chip, core] + swap_in[cc, chip].astype(jnp.float32)
        for rel in range(7):
            total = total + part_in[cc, rel].astype(jnp.float32)
        counts = total[:, STEP * WIDE :]
        weight = counts / (counts + 4.0)
        safe = jnp.maximum(counts, 1.0)
        old = old_ref[cc].astype(jnp.float32)
        fresh = []
        for j in range(STEP):
            lanes = slice(j * WIDE, (j + 1) * WIDE)
            base = old[:, lanes]
            fresh.append(base + weight * (total[:, lanes] / safe - base))
        t_ref[chip, core, :, cc * STEP * WIDE : (cc + 1) * STEP * WIDE] = jnp.concatenate(
            fresh, axis=1
        ).astype(jnp.bfloat16)
        for c in gives[cc]:
            c.start()
        passes[cc][0].start()

    def spread(cc):
        for rel in range(1, 8):
            gives[cc][rel - 1].wait_recv()
            passes[cc][rel].start()

    def settle(cc):
        for c in passes[cc]:
            c.wait_recv()

    for cc in range(CHUNKS):
        gather(cc, 0)
        forward_one(cc)
        if cc + 1 < CHUNKS:
            own_sends(cc + 1)
        gather(cc, 1)
        gather(cc, 2)
        gather(cc, 3)
        if cc >= 1:
            refine(cc - 1)
        forward_two(cc)
        gather(cc, 4)
        finish(cc)
        halos[cc].start()
        gather(cc, 5)
        gather(cc, 6)
        gather(cc, 7)
        merge_labels(cc)
        if cc >= 1:
            spread(cc - 1)
        reduce_start(cc)
    refine(CHUNKS - 1)
    spread(CHUNKS - 1)
    for cc in range(CHUNKS):
        settle(cc)
        halos[cc].wait_recv()

    @pl.when(t == 15)
    def _():
        x_ref[1024 : 1024 + TAIL, :] = jnp.zeros((TAIL, x_ref.shape[1]), jnp.bfloat16)

    want = lax.broadcasted_iota(jnp.int32, (WIDE, 128), 0) - t * 24
    place = lax.broadcasted_iota(jnp.int32, (WIDE, 128), 1)
    chosen = [
        jnp.where(jnp.logical_and(want + cc * WIDE == place, place < 24), 1.0, 0.0).astype(
            jnp.bfloat16
        )
        for cc in range(CHUNKS)
    ]
    for j in range(STEP):
        acc = None
        for cc in range(CHUNKS):
            lane = (cc * STEP + j) * WIDE
            piece = t_ref[:, :, :, lane : lane + WIDE].reshape(256, WIDE)
            piece = dot_f32(piece, chosen[cc])
            acc = piece if acc is None else acc + piece
        v_ref[j] = acc.astype(jnp.bfloat16)

    for c in tab_cp:
        c.wait_send()
    for cc in range(CHUNKS):
        for c in hops[cc] + [halos[cc], swaps[cc]] + scatters[cc] + gives[cc] + passes[cc]:
            c.wait_send()


def exchange(own, tab, old):
    bf16, f32 = jnp.bfloat16, jnp.float32
    dma = pltpu.SemaphoreType.DMA
    vmem = pl.BlockSpec(memory_space=pltpu.VMEM)
    return pl.pallas_call(
        exchange_kernel,
        out_shape=(
            jax.ShapeDtypeStruct((ROWS, CHUNKS * PHASES * WIDE), bf16),
            jax.ShapeDtypeStruct((8, 2, 16, CHUNKS * STEP * WIDE), bf16),
            jax.ShapeDtypeStruct((STEP, 256, 128), bf16),
        ),
        in_specs=[vmem] * 3,
        out_specs=[vmem] * 3,
        scratch_shapes=[
            pltpu.VMEM((8, CAP, 128), jnp.int32),
            pltpu.VMEM((8, GROUPS * STEP * CAP, 1024), bf16),
            pltpu.VMEM((GROUPS, 64, STEP * WIDE), f32),
            pltpu.VMEM((CHUNKS, 8, 2, 16, FLAT * WIDE), f32),
            pltpu.VMEM((CHUNKS, 8, 16, FLAT * WIDE), bf16),
            pltpu.VMEM((CHUNKS, 8, 16, FLAT * WIDE), bf16),
            pltpu.VMEM((CHUNKS, 8, 16, FLAT * WIDE), bf16),
            pltpu.VMEM((CHUNKS, 7, 16, FLAT * WIDE), bf16),
            dma((7,)),
            dma((7,)),
            dma((CHUNKS * 8,)),
            dma((CHUNKS * 8,)),
            dma((CHUNKS,)),
            dma((CHUNKS,)),
            dma((CHUNKS,)),
            dma((CHUNKS,)),
            dma((CHUNKS * 7,)),
            dma((CHUNKS * 7,)),
            dma((CHUNKS * 7,)),
            dma((CHUNKS * 7,)),
            dma((CHUNKS * 8,)),
            dma((CHUNKS * 8,)),
        ],
        compiler_params=pltpu.CompilerParams(
            collective_id=0, has_side_effects=True, vmem_limit_bytes=56 << 20
        ),
        name="exchange",
    )(own, tab, old)


def correlate_kernel(scale, x_ref, t_ref, out_ref, y_ref, rows_ref):
    size = ROWS // 2
    for d in range(4):

        def one(i, carry):
            first = pl.multiple_of(i * size, 16)
            for e in range(3):
                low = max(0, 8 * e - 2 * d)
                high = min(STEP, 8 * e + 8 - 2 * d)
                if low >= high:
                    continue
                total = None
                for cc in range(CHUNKS):
                    p = 2 * d + low - 8 * e
                    xl = (cc * PHASES + p) * WIDE
                    tl = (cc * STEP + low) * WIDE
                    span = (high - low) * WIDE
                    part = dot_nt(
                        x_ref[pl.ds(first, size), xl : xl + span], t_ref[:, tl : tl + span]
                    )
                    total = part if total is None else total + part
                y_ref[e, pl.ds(first, size), :] = total
            return carry

        lax.fori_loop(0, 2, one, 0)
        a = y_ref[0, 0:1032, 0:128] + y_ref[0, 4 : 4 + 1032, 128:256]
        for e in (1, 2) if d > 0 else (1,):
            a = a + y_ref[e, e : e + 1032, 0:128] + y_ref[e, e + 4 : e + 4 + 1032, 128:256]
        f = a[0:1024, 0:64] + a[2 : 2 + 1024, 64:128]
        rows_ref[pl.ds(d, 1024, stride=4), 0:64] = f * scale
    out_ref[...] = rows_ref[...].T[0:64]


def correlate(x, t2, scale):
    vmem = pl.BlockSpec(memory_space=pltpu.VMEM)
    return pl.pallas_call(
        functools.partial(correlate_kernel, scale),
        out_shape=jax.ShapeDtypeStruct((64, 4096), jnp.float32),
        in_specs=[vmem] * 2,
        out_specs=vmem,
        scratch_shapes=[
            pltpu.VMEM((3, ROWS, 256), jnp.float32),
            pltpu.VMEM((4096, 128), jnp.float32),
        ],
        compiler_params=pltpu.CompilerParams(vmem_limit_bytes=48 << 20),
        name="correlate",
    )(x, t2)


def body(recording, spike_times, unit_labels, old_templates):
    sub_rows, chans = recording.shape
    panel, feat = old_templates.shape
    spikes = spike_times.shape[0]
    t = lax.axis_index("tm")
    u = lax.axis_index("unit")
    start = spike_times - (t * 8 + u) * sub_rows - (TAPS - 1) // 2
    owner = unit_labels // panel
    within = unit_labels % panel
    before = jnp.arange(spikes)[None, :] < jnp.arange(spikes)[:, None]
    rank = jnp.sum(
        jnp.logical_and(owner[:, None] == owner[None, :], before).astype(jnp.int32), axis=1
    )
    slot = owner * CAP + rank
    hit = jnp.arange(8 * CAP)[:, None] == slot[None, :]
    start_of = jnp.sum(jnp.where(hit, start[None, :], 0), axis=1)
    label_of = jnp.sum(jnp.where(hit, within[None, :] + 1, 0), axis=1) - 1
    lane = jnp.arange(128)[None, :]
    tab = jnp.where(lane < 64, start_of[:, None], label_of[:, None]).reshape(8, CAP, 128)

    rows = lax.dynamic_slice_in_dim(old_templates, (t % 4) * 16, 16, 0)
    rows = rows.reshape(16, chans, TAPS)
    rows = jnp.pad(rows, ((0, 0), (0, 0), (0, GROUPS * STEP - TAPS)))
    rows = lax.dynamic_slice_in_dim(rows, (t // 4) * STEP, STEP, 2)
    old = rows.reshape(16, CHUNKS, WIDE, STEP).transpose(1, 0, 3, 2)
    old = old.reshape(CHUNKS, 16, STEP * WIDE)

    x, t2, v = exchange(recording, tab.astype(jnp.int32), old)
    scale = 1.0 / (feat**0.5)
    scores = correlate(x, t2.reshape(256, CHUNKS * STEP * WIDE), scale)
    share = chans // 16
    v = v[:, :, :share].reshape(STEP, GROUPS, panel, share).transpose(2, 3, 1, 0)
    templates = v.reshape(panel, share, GROUPS * STEP)[:, :, :TAPS].reshape(panel, share * TAPS)
    return (templates, scores)


def solution(mesh):
    in_specs = (P(("tm", "unit"), None), P(("tm", "unit")), P(("tm", "unit")), P("unit", None))
    out_specs = (P("unit", "tm"), P("unit", "tm"))
    return jax.shard_map(body, mesh=mesh, in_specs=in_specs, out_specs=out_specs, check_vma=False)
```

time: 509 us -> 161 us (0.32)
  waiting for transfers between devices: 221 us -> 0 us
  Pallas kernels: 0 us -> 138 us
  local copies, waits for them, and re-layouts: 136 us -> 20 us
  matrix products: 64.7 us -> 0 us
  blocking collectives: 33.7 us -> 0 us
  starting transfers between devices: 17.2 us -> 0 us
  other arithmetic: 17.5 us -> 1.82 us
  between operations: 15.6 us -> 0.73 us
    psum x1 -> x0, waiting for transfers between devices: 185 us -> none  [body(): total_sums, total_counts = lax.psum((sums, counts), 'tm')]
    pallas_call x0 -> x2, Pallas kernels: none -> 138 us  [the longest x1 117 us: exchange(): pl.pallas_call(exchange_kernel, out_shape=(jax.ShapeDtypeStruct((ROWS, CH...]
    gather x96 -> x0, local copies, waits for them, and re-layouts: 85.4 us -> none
    conv_general_dilated x1 -> x0, matrix products: 56.5 us -> none  [correlate(): lax.conv_general_dilated(extended[None], kernel, (STRIDE,), 'VALID', dime...]
    all_to_all x2 -> x0, waiting for transfers between devices: 35.6 us -> none  [the longest x1 35.6 us: body(): lax.all_to_all(send_rows, 'unit', split_axis=0, concat_axis=0, tiled=True)]
    psum x1 -> x0, blocking collectives: 33.7 us -> none  [body(): total_sums, total_counts = lax.psum((sums, counts), 'tm')]
    reshape x3 -> x6, local copies, waits for them, and re-layouts: 32.4 us -> 13.8 us  [the longest x1 6.57 us: body(): rows = rows.reshape(16, chans, TAPS)]
    all_to_all x2 -> x0, starting transfers between devices: 11.9 us -> none  [the longest x1 6.79 us: body(): lax.all_to_all(send_tags, 'unit', split_axis=0, concat_axis=0, tiled=True)]
  transfers between devices with their start and end apart: 5 -> 0, of which waited for: 2 -> 0; matrix products, arithmetic and copies ran while one was open for 26% -> 0% of each run, Pallas kernels for 0% -> 0%
where the time goes in v1:
time: 161 us; the launch traced here: 160 us
  Pallas kernels  138 us (86%)
  local copies, waits for them, and re-layouts  20 us (12%)
  other arithmetic  1.82 us (1%)
    pallas_call x1, Pallas kernels, exchange(): pl.pallas_call(exchange_kernel, out_shape=(jax.ShapeDtypeStruct((ROWS, CH...  117 us
    pallas_call x1, Pallas kernels, correlate(): pl.pallas_call(functools.partial(correlate_kernel, scale), out_shape=jax....  20.8 us
    reshape x1, local copies, waits for them, and re-layouts, body(): rows = rows.reshape(16, chans, TAPS)  6.57 us

profile of v1, /device:TPU:1, one launch (start us, length us, event | category | flops | bytes accessed | tf_op | source)
XLA Modules:
  0.0 160.3 jit_solution(7670088130640653093)
XLA Ops:
  0.6 0.0 copy-start
  0.7 0.8 fusion.1
  1.5 0.2 convert_reduce_fusion
  1.7 0.1 select_reduce_fusion.1
  1.8 0.1 sub.31
  1.9 0.1 broadcast_in_dim.58
  2.0 0.7 broadcast_select_fusion.tab_ref
  2.7 0.0 copy-done
  2.7 0.9 constant_dynamic-slice_fusion
  3.6 6.6 %reshape.59 = bf16[16,384,61]{2,1,0:T(8,128)(2,1)} reshape(bf16[16,23424]{1,0:T(8,128)(2,1)} %constant_dynamic-slice_fusion) | data formatting | bytes 1499136 | tf_op jit(solution)/shard_map/reshape | solution.py:490
  10.2 3.2 %pad_dynamic-slice_fusion = bf16[16,384,16]{2,1,0:T(8,128)(2,1)} fusion(s32[]{:T(128)S(6)} %select_n.48, bf16[16,384,61]{2,1,0:T(8,128)(2,1)} %reshape.59), kind=kLoop, calls=%fused_computation | loop fusion | bytes 946180 | tf_op jit(solution)/shard_map/dynamic_slice | solution.py:492
  13.4 1.8 %copy.14 = bf16[16,3,128,16]{2,1,3,0:T(4,128)(2,1)S(1)} copy(bf16[16,3,128,16]{3,2,1,0:T(8,128)(2,1)} %bitcast.14) | data formatting | bytes 393216 | tf_op jit(solution)/shard_map/reshape | solution.py:493
  15.3 0.8 reshape.61.old_ref
  16.0 116.9 %exchange.1 = (bf16[1056,3072]{1,0:T(8,128)(2,1)}, bf16[8,2,16,6144]{3,2,1,0:T(8,128)(2,1)}, bf16[16,256,128]{2,1,0:T(8,128)(2,1)}) custom-call(bf16[1024,384]{1,0:T(8,128)(2,1)} %own_ref.1, s32[8,8,128]{2,1,0:T(8,128)} %broadcast_select_fusion.tab_ref, bf16[3,16,2048]{2,1,0:T(8,128)(2,1)} %reshape.61.old_ref), custom_call_target="tpu_custom_call" | custom-call | tf_op jit(solution)/shard_map/exchange/pallas_call | solution.py:380
  132.9 1.9 %copy.12 = bf16[16,4,64,24]{2,0,1,3:T(8,128)(2,1)S(1)} copy(bf16[16,4,64,24]{3,2,1,0:T(8,128)(2,1)} %bitcast.17) | data formatting | bytes 393216 | tf_op jit(solution)/shard_map/reshape | solution.py:500
  134.9 0.9 reshape.66
  135.7 1.9 %copy.15 = bf16[64,1464]{1,0:T(8,128)(2,1)} copy(bf16[64,1464]{0,1:T(8,128)(2,1)} %reshape.66) | data formatting | bytes 374784 | tf_op jit(solution)/shard_map/reshape | solution.py:501
  137.6 0.0 copy-start.1
  137.6 1.9 %copy-done.1 = bf16[8,2,16,6144]{3,2,1,0:T(8,128)(2,1)S(1)} copy-done((bf16[8,2,16,6144]{3,2,1,0:T(8,128)(2,1)S(1)}, bf16[8,2,16,6144]{3,2,1,0:T(8,128)(2,1)}, u32[]{:S(2)}) %copy-start.1) | copy-done | bytes 3145752
  139.5 20.8 %correlate.1 = f32[64,4096]{1,0:T(8,128)} custom-call(bf16[1056,3072]{1,0:T(8,128)(2,1)} %get-tuple-element.6.x_ref, bf16[256,6144]{1,0:T(8,128)(2,1)S(1)} %bitcast.13), custom_call_target="tpu_custom_call" | custom-call | tf_op jit(solution)/shard_map/correlate/pallas_call | solution.py:455
  (4 shorter events, 0.0 us)
Async XLA Ops:
  0.6 2.1 %copy-start = (bf16[64,23424]{1,0:T(8,128)(2,1)S(1)}, bf16[64,23424]{1,0:T(8,128)(2,1)}, u32[]{:S(2)}) copy-start(bf16[64,23424]{1,0:T(8,128)(2,1)} %param.7) | copy-start | bytes 8994820
  137.6 1.9 %copy-start.1 = (bf16[8,2,16,6144]{3,2,1,0:T(8,128)(2,1)S(1)}, bf16[8,2,16,6144]{3,2,1,0:T(8,128)(2,1)}, u32[]{:S(2)}) copy-start(bf16[8,2,16,6144]{3,2,1,0:T(8,128)(2,1)} %get-tuple-element.7) | copy-start | bytes 9437188

commit v2 on v1

v2 whole, which is shorter than its diff:
```python
import functools

import jax
import jax.numpy as jnp
from jax import lax
from jax.experimental import pallas as pl
from jax.experimental.pallas import tpu as pltpu
from jax.sharding import PartitionSpec as P

MESH = pl.DeviceIdType.MESH
TAPS = 61
CAP = 8
GROUPS = 4
STEP = 16
PHASES = 8
LINES = 128
ROWS = 1056
TAIL = 16
CHUNKS = 3
WIDE = 128
FLAT = STEP + 1
SIZE = ROWS // 2
LONG = TAPS * WIDE


def dot_f32(a, b):
    return jnp.dot(a, b, preferred_element_type=jnp.float32)


def dot_nt(a, b):
    return lax.dot_general(a, b, (((1,), (1,)), ((), ())), preferred_element_type=jnp.float32)


PLANES = [(d, e) for d in range(4) for e in range(3 if d > 0 else 2)]


def refine_kernel(
    scale,
    own_ref,
    tab_ref,
    old_ref,
    new_ref,
    score_ref,
    x_ref,
    t_ref,
    old_rows,
    old_tall,
    old_wide,
    tabs,
    picks,
    snip,
    sums,
    away,
    swap_in,
    part,
    part_in,
    keep,
    side_out,
    side_in,
    y_ref,
    rows_ref,
    new_tall,
    old_s,
    tab_s,
    tab_r,
    ag_s,
    ag_r,
    halo_s,
    halo_r,
    swap_s,
    swap_r,
    ys_s,
    ys_r,
    xs_s,
    xs_r,
    xg_s,
    xg_r,
    yg_s,
    yg_r,
    fw_s,
    fw_r,
):
    t = lax.axis_index("tm")
    u = lax.axis_index("unit")
    core = lax.rem(t, 2)
    chip = t // 2
    yy = chip // 2
    xh = lax.rem(chip, 2)
    beside = yy * 2 + 1 - xh
    z = lax.rem(u, 4)
    side = u - z
    other = 4 - side
    zp = lax.rem(z + 1, 4)
    zm = lax.rem(z + 3, 4)
    zo = lax.rem(z + 2, 4)
    up, down, across = side + zp, side + zm, other + z

    ug = lax.rem(t, 4)
    tg = t // 4
    old_cp = pltpu.make_async_copy(
        old_ref.at[pl.ds(pl.multiple_of(ug * 16, 16), 16)], old_rows, old_s
    )
    old_cp.start()

    barrier = pltpu.get_barrier_semaphore()
    for rel in range(1, 8):
        pl.semaphore_signal(
            barrier, inc=1, device_id={"unit": lax.rem(u + rel, 8)}, device_id_type=MESH
        )
    for rel in range(1, 16):
        pl.semaphore_signal(
            barrier, inc=1, device_id={"tm": lax.rem(t + rel, 16)}, device_id_type=MESH
        )
    pl.semaphore_wait(barrier, 22)

    row = lax.broadcasted_iota(jnp.int32, (LINES, 1024), 0) * PHASES
    col = lax.broadcasted_iota(jnp.int32, (LINES, 1024), 1)
    mine = pl.ds(pl.multiple_of(u * LINES, LINES), LINES)

    def sort_phases(first, last):
        own = own_ref[:, first * WIDE : last * WIDE]
        for p in range(PHASES):
            pick = jnp.where(col == row + p, 1.0, 0.0).astype(jnp.bfloat16)
            got = dot_f32(pick, own).astype(jnp.bfloat16)
            for cc in range(first, last):
                lane = (cc * PHASES + p) * WIDE
                x_ref[mine, lane : lane + WIDE] = got[
                    :, (cc - first) * WIDE : (cc - first + 1) * WIDE
                ]

    def block(index, cc, first=0, count=LINES):
        return x_ref.at[
            pl.ds(pl.multiple_of(index * LINES + first, 16), count),
            cc * PHASES * WIDE : (cc + 1) * PHASES * WIDE,
        ]

    def remote(src, dst, send, recv, where):
        return pltpu.make_async_remote_copy(
            src_ref=src,
            dst_ref=dst,
            send_sem=send,
            recv_sem=recv,
            device_id=where,
            device_id_type=MESH,
        )

    def hop(cc, k, ref, to):
        return remote(ref, ref, ag_s.at[cc * 8 + k], ag_r.at[cc * 8 + k], {"unit": to})

    half = LINES // 2
    hops = [
        [
            hop(cc, 0, block(u, cc), across),
            hop(cc, 1, block(u, cc), up),
            hop(cc, 2, block(u, cc), down),
            hop(cc, 3, block(down, cc, 0, half), up),
            hop(cc, 4, block(up, cc, half, half), down),
            hop(cc, 5, block(across, cc), up),
            hop(cc, 6, block(across, cc), down),
            hop(cc, 7, block(side + zo, cc), across),
        ]
        for cc in range(CHUNKS)
    ]

    def own_sends(cc):
        for k in (0, 1, 2):
            hops[cc][k].start()

    def forward_one(cc):
        hops[cc][0].wait_recv()
        hops[cc][5].start()
        hops[cc][6].start()
        hops[cc][1].wait_recv()
        hops[cc][3].start()
        hops[cc][2].wait_recv()
        hops[cc][4].start()

    def forward_two(cc):
        hops[cc][3].wait_recv()
        hops[cc][4].wait_recv()
        hops[cc][7].start()

    def finish(cc):
        hops[cc][5].wait_recv()
        hops[cc][6].wait_recv()
        hops[cc][7].wait_recv()
        halos[cc].start()

    def halo(cc):
        lanes = pl.ds(cc * PHASES * WIDE, PHASES * WIDE)
        return remote(
            x_ref.at[pl.ds(0, TAIL), lanes],
            x_ref.at[pl.ds(1024, TAIL), lanes],
            halo_s.at[cc],
            halo_r.at[cc],
            {"tm": lax.rem(t + 15, 16)},
        )

    halos = [halo(cc) for cc in range(CHUNKS)]

    sort_phases(0, 1)
    own_sends(0)
    tab_cp = []
    for rel in range(1, 8):
        to = lax.rem(u + rel, 8)
        c = remote(
            tab_ref.at[to], tabs.at[u], tab_s.at[rel - 1], tab_r.at[rel - 1], {"unit": to}
        )
        c.start()
        tab_cp.append(c)
    sort_phases(1, CHUNKS)
    tabs[u] = tab_ref[u]
    for c in tab_cp:
        c.wait_recv()

    tval = lax.broadcasted_iota(jnp.int32, (CAP, 1024), 1)
    tval = (tval % LINES) * PHASES + tval // LINES
    lead = lax.broadcasted_iota(jnp.int32, (GROUPS * STEP, 1, 1), 0)
    tap = (lead % GROUPS) * STEP + lead // GROUPS
    tap = jnp.where(tap < TAPS, tap, -100000)
    order = [u, across, up, down, side + zo, other + zp, other + zm, other + zo]

    def build_picks(i, carry):
        start = tabs[i][:, 0:1]
        gap = (tval - start)[None]
        pick = jnp.where(gap == tap, 1.0, 0.0).reshape(GROUPS * STEP * CAP, 1024)
        picks[i] = pick.astype(jnp.bfloat16)
        return carry

    lax.fori_loop(0, 8, build_picks, 0)

    labels = tabs[...].reshape(64, 128)[:, 64:65]
    labels = jnp.concatenate([labels] * GROUPS, axis=0)
    r4 = lax.broadcasted_iota(jnp.int32, (256, 256), 0)
    c4 = lax.broadcasted_iota(jnp.int32, (256, 256), 1)
    merge = jnp.where(
        jnp.logical_and(labels == c4 % 64, r4 // 64 == c4 // 64), 1.0, 0.0
    )
    merge = merge.T.astype(jnp.bfloat16)
    tally = dot_f32(merge, jnp.ones((256, WIDE), jnp.bfloat16))

    def relay_old():
        old_cp.wait()
        for cc in range(CHUNKS):

            def turn(i, carry):
                src = pl.ds(pl.multiple_of(cc * LONG + i * 128, 128), 128)
                at = pl.ds(pl.multiple_of(i * 128, 128), 128)
                old_tall[at, :] = old_rows[:, src].astype(jnp.float32).T
                return carry

            lax.fori_loop(0, TAPS, turn, 0)
            for j in range(STEP):
                piece = old_tall[pl.ds(tg * STEP + j, WIDE, stride=TAPS), :].T
                piece = jnp.where(tg * STEP + j < TAPS, piece, 0.0)
                old_wide[cc, :, j * WIDE : (j + 1) * WIDE] = piece

    def gather(cc, position):
        b = order[position]
        base = cc * PHASES * WIDE
        rows = pl.ds(pl.multiple_of(b * LINES, LINES), LINES)
        data = jnp.concatenate(
            [x_ref[rows, base + p * WIDE : base + (p + 1) * WIDE] for p in range(PHASES)],
            axis=0,
        )
        cut = dot_f32(picks[b], data)
        at = pl.ds(pl.multiple_of(b * CAP, CAP), CAP)
        for j in range(STEP):
            for g in range(GROUPS):
                r = (j * GROUPS + g) * CAP
                snip[g, at, j * WIDE : (j + 1) * WIDE] = cut[r : r + CAP]

    swaps = [
        remote(away, swap_in.at[cc], swap_s.at[cc], swap_r.at[cc], {"tm": chip * 2 + 1 - core})
        for cc in range(CHUNKS)
    ]

    def merge_labels(cc):
        if cc > 0:
            swaps[cc - 1].wait_send()
        out = dot_f32(merge, snip[...].reshape(256, STEP * WIDE).astype(jnp.bfloat16))
        out = jnp.concatenate([out, tally], axis=1).reshape(4, 2, 2, 16, FLAT * WIDE)
        sums[...] = out
        away[...] = sums[:, :, 1 - core]
        swaps[cc].start()

    def y_send(cc, rel):
        to = lax.rem(yy + rel, 4)
        return remote(
            part.at[cc, to],
            part_in.at[cc, rel - 1],
            ys_s.at[cc * 3 + rel - 1],
            ys_r.at[cc * 3 + rel - 1],
            {"tm": (to * 2 + xh) * 2 + core},
        )

    y_sends = [[y_send(cc, rel) for rel in (1, 2, 3)] for cc in range(CHUNKS)]
    x_sends = [
        remote(side_out.at[cc], side_in.at[cc], xs_s.at[cc], xs_r.at[cc], {"tm": beside * 2 + core})
        for cc in range(CHUNKS)
    ]

    def reduce_one(cc):
        swaps[cc].wait_recv()
        both = sums[:, :, core] + swap_in[cc]
        part[cc] = both.astype(jnp.bfloat16)
        for c in y_sends[cc]:
            c.start()
        sums[:, :, core] = both

    def reduce_two(cc):
        for c in y_sends[cc]:
            c.wait_recv()
        far = sums[yy, 1 - xh, core]
        near = sums[yy, xh, core]
        for rel in range(3):
            far = far + part_in[cc, rel, 1 - xh].astype(jnp.float32)
            near = near + part_in[cc, rel, xh].astype(jnp.float32)
        side_out[cc] = far.astype(jnp.bfloat16)
        x_sends[cc].start()
        keep[cc] = near

    def panel(cc, ch, co):
        return t_ref.at[ch, co, :, cc * STEP * WIDE : (cc + 1) * STEP * WIDE]

    def x_give(cc):
        ref = panel(cc, chip, core)
        return remote(ref, ref, xg_s.at[cc], xg_r.at[cc], {"tm": beside * 2 + core})

    def y_give(cc, rel, ch, k):
        ref = panel(cc, ch, core)
        to = lax.rem(yy + rel, 4)
        return remote(
            ref,
            ref,
            yg_s.at[cc * 6 + k * 3 + rel - 1],
            yg_r.at[cc * 6 + k * 3 + rel - 1],
            {"tm": (to * 2 + xh) * 2 + core},
        )

    def pass_on(cc, k, ch):
        ref = panel(cc, ch, core)
        return remote(
            ref, ref, fw_s.at[cc * 8 + k], fw_r.at[cc * 8 + k], {"tm": chip * 2 + 1 - core}
        )

    x_gives = [x_give(cc) for cc in range(CHUNKS)]
    y_gives = [
        [y_give(cc, rel, ch, k) for k, ch in ((0, chip), (1, beside)) for rel in (1, 2, 3)]
        for cc in range(CHUNKS)
    ]
    origin = [chip, beside]
    for half_x in (xh, 1 - xh):
        for rel in (1, 2, 3):
            origin.append(lax.rem(yy + 4 - rel, 4) * 2 + half_x)
    passes = [[pass_on(cc, k, origin[k]) for k in range(8)] for cc in range(CHUNKS)]

    def refine(cc):
        x_sends[cc].wait_recv()
        total = keep[cc] + side_in[cc].astype(jnp.float32)
        counts = total[:, STEP * WIDE :]
        weight = counts / (counts + 4.0)
        safe = jnp.maximum(counts, 1.0)
        fresh = []
        for j in range(STEP):
            lanes = slice(j * WIDE, (j + 1) * WIDE)
            base = old_wide[cc, :, lanes]
            fresh.append(base + weight * (total[:, lanes] / safe - base))
        t_ref[chip, core, :, cc * STEP * WIDE : (cc + 1) * STEP * WIDE] = jnp.concatenate(
            fresh, axis=1
        ).astype(jnp.bfloat16)
        x_gives[cc].start()
        for c in y_gives[cc][:3]:
            c.start()
        passes[cc][0].start()

    def spread_one(cc):
        x_gives[cc].wait_recv()
        for c in y_gives[cc][3:]:
            c.start()
        passes[cc][1].start()

    def spread_two(cc):
        for k in range(6):
            y_gives[cc][k].wait_recv()
            passes[cc][2 + k].start()

    def settle(cc):
        for c in passes[cc]:
            c.wait_recv()
        halos[cc].wait_recv()

        @pl.when(t == 15)
        def _():
            x_ref[1024 : 1024 + TAIL, cc * PHASES * WIDE : (cc + 1) * PHASES * WIDE] = jnp.zeros(
                (TAIL, PHASES * WIDE), jnp.bfloat16
            )

    def correlate(cc, d):
        def one(i, carry):
            first = pl.multiple_of(i * SIZE, 16)
            for at, (dd, e) in enumerate(PLANES):
                if dd != d:
                    continue
                low = max(0, 8 * e - 2 * d)
                high = min(STEP, 8 * e + 8 - 2 * d)
                xl = (cc * PHASES + 2 * d + low - 8 * e) * WIDE
                tl = (cc * STEP + low) * WIDE
                span = (high - low) * WIDE
                panels = t_ref[:, :, :, tl : tl + span].reshape(256, span)
                total = dot_nt(x_ref[pl.ds(first, SIZE), xl : xl + span], panels)
                if cc == 0:
                    y_ref[at, pl.ds(first, SIZE), :] = total
                else:
                    y_ref[at, pl.ds(first, SIZE), :] += total
            return carry

        lax.fori_loop(0, 2, one, 0)

    def collect(d):
        a = None
        for at, (dd, e) in enumerate(PLANES):
            if dd != d:
                continue
            b = y_ref[at, e : e + 1032, 0:128] + y_ref[at, e + 4 : e + 4 + 1032, 128:256]
            a = b if a is None else a + b
        f = a[0:1024, 0:64] + a[2 : 2 + 1024, 64:128]
        rows_ref[pl.ds(d, 1024, stride=4), 0:64] = f * scale

    def write_new():
        want = lax.broadcasted_iota(jnp.int32, (32, WIDE), 1) - t * 24
        place = lax.broadcasted_iota(jnp.int32, (32, WIDE), 0)
        chosen = [
            jnp.where(jnp.logical_and(want + cc * WIDE == place, place < 24), 1.0, 0.0).astype(
                jnp.bfloat16
            )
            for cc in range(CHUNKS)
        ]
        for j in range(STEP):
            acc = None
            for cc in range(CHUNKS):
                lane = (cc * STEP + j) * WIDE
                piece = t_ref[:, :, :, lane : lane + WIDE].reshape(256, WIDE)
                piece = dot_nt(chosen[cc], piece)
                acc = piece if acc is None else acc + piece
            for g in range(GROUPS):
                if g * STEP + j < TAPS:
                    new_tall[pl.ds(g * STEP + j, 24, stride=TAPS), 0:64] = acc[
                        0:24, g * 64 : (g + 1) * 64
                    ]
        new_ref[...] = new_tall[...].T[0:64, 0 : 24 * TAPS].astype(jnp.bfloat16)

    relay_old()

    forward_one(0)
    own_sends(1)
    for q in range(4):
        gather(0, q)
    forward_two(0)
    gather(0, 4)
    finish(0)
    for q in (5, 6, 7):
        gather(0, q)
    merge_labels(0)

    forward_one(1)
    own_sends(2)
    reduce_one(0)
    for q in range(4):
        gather(1, q)
    forward_two(1)
    gather(1, 4)
    reduce_two(0)
    finish(1)
    refine(0)
    for q in (5, 6, 7):
        gather(1, q)
    merge_labels(1)

    forward_one(2)
    spread_one(0)
    reduce_one(1)
    for q in range(4):
        gather(2, q)
    forward_two(2)
    gather(2, 4)
    reduce_two(1)
    spread_two(0)
    finish(2)
    refine(1)
    for q in (5, 6, 7):
        gather(2, q)
    merge_labels(2)

    spread_one(1)
    settle(0)
    correlate(0, 0)
    reduce_one(2)
    correlate(0, 1)
    spread_two(1)
    correlate(0, 2)
    correlate(0, 3)
    reduce_two(2)
    settle(1)
    correlate(1, 0)
    refine(2)
    correlate(1, 1)
    spread_one(2)
    correlate(1, 2)
    correlate(1, 3)
    spread_two(2)
    settle(2)
    for d in range(4):
        correlate(2, d)
        collect(d)
    score_ref[...] = rows_ref[...].T[0:64]
    write_new()

    for c in tab_cp:
        c.wait_send()
    swaps[CHUNKS - 1].wait_send()
    for cc in range(CHUNKS):
        for c in hops[cc] + [halos[cc], x_sends[cc], x_gives[cc]]:
            c.wait_send()
        for c in y_sends[cc] + y_gives[cc] + passes[cc]:
            c.wait_send()


def refine_and_correlate(own, tab, old, scale):
    bf16, f32 = jnp.bfloat16, jnp.float32
    dma = pltpu.SemaphoreType.DMA
    vmem = pl.BlockSpec(memory_space=pltpu.VMEM)
    flat = FLAT * WIDE
    return pl.pallas_call(
        functools.partial(refine_kernel, scale),
        out_shape=(
            jax.ShapeDtypeStruct((64, 24 * TAPS), bf16),
            jax.ShapeDtypeStruct((64, 4096), f32),
        ),
        in_specs=[vmem, vmem, pl.BlockSpec(memory_space=pl.ANY)],
        out_specs=[vmem] * 2,
        scratch_shapes=[
            pltpu.VMEM((ROWS, CHUNKS * PHASES * WIDE), bf16),
            pltpu.VMEM((8, 2, 16, CHUNKS * STEP * WIDE), bf16),
            pltpu.VMEM((16, CHUNKS * LONG), bf16),
            pltpu.VMEM((LONG + 64, 16), f32),
            pltpu.VMEM((CHUNKS, 16, STEP * WIDE), f32),
            pltpu.VMEM((8, CAP, 128), jnp.int32),
            pltpu.VMEM((8, GROUPS * STEP * CAP, 1024), bf16),
            pltpu.VMEM((GROUPS, 64, STEP * WIDE), f32),
            pltpu.VMEM((4, 2, 2, 16, flat), f32),
            pltpu.VMEM((4, 2, 16, flat), f32),
            pltpu.VMEM((CHUNKS, 4, 2, 16, flat), f32),
            pltpu.VMEM((CHUNKS, 4, 2, 16, flat), bf16),
            pltpu.VMEM((CHUNKS, 3, 2, 16, flat), bf16),
            pltpu.VMEM((CHUNKS, 16, flat), f32),
            pltpu.VMEM((CHUNKS, 16, flat), bf16),
            pltpu.VMEM((CHUNKS, 16, flat), bf16),
            pltpu.VMEM((len(PLANES), ROWS, 256), f32),
            pltpu.VMEM((4096, 128), f32),
            pltpu.VMEM((1536, 128), f32),
            dma,
            dma((7,)),
            dma((7,)),
            dma((CHUNKS * 8,)),
            dma((CHUNKS * 8,)),
            dma((CHUNKS,)),
            dma((CHUNKS,)),
            dma((CHUNKS,)),
            dma((CHUNKS,)),
            dma((CHUNKS * 3,)),
            dma((CHUNKS * 3,)),
            dma((CHUNKS,)),
            dma((CHUNKS,)),
            dma((CHUNKS,)),
            dma((CHUNKS,)),
            dma((CHUNKS * 6,)),
            dma((CHUNKS * 6,)),
            dma((CHUNKS * 8,)),
            dma((CHUNKS * 8,)),
        ],
        compiler_params=pltpu.CompilerParams(
            collective_id=0, has_side_effects=True, vmem_limit_bytes=62 << 20
        ),
        name="refine_and_correlate",
    )(own, tab, old)


def body(recording, spike_times, unit_labels, old_templates):
    sub_rows = recording.shape[0]
    panel, feat = old_templates.shape
    spikes = spike_times.shape[0]
    t = lax.axis_index("tm")
    u = lax.axis_index("unit")
    start = spike_times - (t * 8 + u) * sub_rows - (TAPS - 1) // 2
    owner = unit_labels // panel
    within = unit_labels % panel
    before = jnp.arange(spikes)[None, :] < jnp.arange(spikes)[:, None]
    rank = jnp.sum(
        jnp.logical_and(owner[:, None] == owner[None, :], before).astype(jnp.int32), axis=1
    )
    slot = owner * CAP + rank
    hit = jnp.arange(8 * CAP)[:, None] == slot[None, :]
    start_of = jnp.sum(jnp.where(hit, start[None, :], 0), axis=1)
    label_of = jnp.sum(jnp.where(hit, within[None, :] + 1, 0), axis=1) - 1
    lane = jnp.arange(128)[None, :]
    tab = jnp.where(lane < 64, start_of[:, None], label_of[:, None]).reshape(8, CAP, 128)
    scale = 1.0 / (feat**0.5)
    return refine_and_correlate(recording, tab.astype(jnp.int32), old_templates, scale)


def solution(mesh):
    in_specs = (P(("tm", "unit"), None), P(("tm", "unit")), P(("tm", "unit")), P("unit", None))
    out_specs = (P("unit", "tm"), P("unit", "tm"))
    return jax.shard_map(body, mesh=mesh, in_specs=in_specs, out_specs=out_specs, check_vma=False)
```

time: 161 us -> 145 us (0.901)
  local copies, waits for them, and re-layouts: 20 us -> 4.04 us
    reshape x6 -> x0, local copies, waits for them, and re-layouts: 13.8 us -> none  [the longest x1 6.57 us: body(): rows = rows.reshape(16, chans, TAPS)]
    dynamic_slice x2 -> x0, local copies, waits for them, and re-layouts: 4.13 us -> none  [the longest x1 3.22 us: body(): rows = lax.dynamic_slice_in_dim(rows, t // 4 * STEP, STEP, 2)]
    unnamed x4 -> x2, local copies, waits for them, and re-layouts: 1.9 us -> 3.89 us
    pallas_call x2 -> x1, Pallas kernels: 138 us -> 138 us  [refine_and_correlate(): pl.pallas_call(functools.partial(refine_kernel, scale), out_shape=(jax.Sh...]
where the time goes in v2:
time: 145 us; the launch traced here: 144 us
  Pallas kernels  138 us (95%)
  local copies, waits for them, and re-layouts  4.04 us (3%)
  other arithmetic  1.69 us (1%)
    pallas_call x1, Pallas kernels, refine_and_correlate(): pl.pallas_call(functools.partial(refine_kernel, scale), out_shape=(jax.Sh...  138 us
    unnamed x2, local copies, waits for them, and re-layouts  3.89 us

profile of v2, /device:TPU:1, one launch (start us, length us, event | category | flops | bytes accessed | tf_op | source)
XLA Modules:
  0.0 144.3 jit_solution(118905614557000913)
XLA Ops:
  0.6 0.7 fusion.1
  1.3 0.2 convert_reduce_fusion
  1.5 0.1 select_reduce_fusion.1
  1.6 0.1 sub.27
  1.7 0.1 broadcast_in_dim.58
  1.8 0.7 broadcast_select_fusion.tab_ref
  2.5 137.9 %refine_and_correlate.1 = (bf16[64,1464]{1,0:T(8,128)(2,1)}, f32[64,4096]{1,0:T(8,128)}) custom-call(bf16[1024,384]{1,0:T(8,128)(2,1)} %own_ref.1, s32[8,8,128]{2,1,0:T(8,128)} %broadcast_select_fusion.tab_ref, bf16[64,23424]{1,0:T(8,128)(2,1)} %old_ref.1), custom_call_target="tpu_custom_call" | custom-call | tf_op jit(solution)/shard_map/refine_and_correlate/pallas_call | solution.py:534
  140.4 1.6 %copy.8 = bf16[64,1464]{1,0:T(8,128)(2,1)} copy(bf16[64,1464]{1,0:T(8,128)(2,1)} %get-tuple-element.9) | data formatting | bytes 374784
  142.0 2.3 %copy.9 = f32[64,4096]{1,0:T(8,128)} copy(f32[64,4096]{1,0:T(8,128)} %get-tuple-element.10) | data formatting | bytes 2097152
  (3 shorter events, 0.0 us)

commit v3 on v2

--- a/solution.py
+++ b/solution.py
@@ -54,6 +54,8 @@
     swap_in,
     part,
     part_in,
+    via_in,
+    far_in,
     keep,
     side_out,
     side_in,
@@ -111,8 +113,6 @@
         pl.semaphore_signal(
             barrier, inc=1, device_id={"tm": lax.rem(t + rel, 16)}, device_id_type=MESH
         )
-    pl.semaphore_wait(barrier, 22)
-
     row = lax.broadcasted_iota(jnp.int32, (LINES, 1024), 0) * PHASES
     col = lax.broadcasted_iota(jnp.int32, (LINES, 1024), 1)
     mine = pl.ds(pl.multiple_of(u * LINES, LINES), LINES)
@@ -145,45 +145,65 @@
         )
 
     def hop(cc, k, ref, to):
-        return remote(ref, ref, ag_s.at[cc * 8 + k], ag_r.at[cc * 8 + k], {"unit": to})
+        return remote(ref, ref, ag_s.at[cc * 14 + k], ag_r.at[cc * 14 + k], {"unit": to})
 
     half = LINES // 2
-    hops = [
-        [
-            hop(cc, 0, block(u, cc), across),
-            hop(cc, 1, block(u, cc), up),
-            hop(cc, 2, block(u, cc), down),
-            hop(cc, 3, block(down, cc, 0, half), up),
-            hop(cc, 4, block(up, cc, half, half), down),
-            hop(cc, 5, block(across, cc), up),
-            hop(cc, 6, block(across, cc), down),
-            hop(cc, 7, block(side + zo, cc), across),
+
+    def plan(cc):
+        def low(index):
+            return block(index, cc, 0, half)
+
+        def high(index):
+            return block(index, cc, half, half)
+
+        pairs = [
+            (low(u), across),
+            (high(u), across),
+            (low(u), up),
+            (high(u), up),
+            (low(u), down),
+            (high(u), down),
+            (low(down), up),
+            (high(up), down),
+            (low(across), up),
+            (low(across), down),
+            (high(across), up),
+            (high(across), down),
+            (low(side + zo), across),
+            (high(side + zo), across),
         ]
-        for cc in range(CHUNKS)
-    ]
+        return [hop(cc, k, ref, to) for k, (ref, to) in enumerate(pairs)]
+
+    hops = [plan(cc) for cc in range(CHUNKS)]
 
     def own_sends(cc):
-        for k in (0, 1, 2):
+        for k in (2, 5, 0, 3, 4, 1):
             hops[cc][k].start()
 
-    def forward_one(cc):
-        hops[cc][0].wait_recv()
-        hops[cc][5].start()
-        hops[cc][6].start()
-        hops[cc][1].wait_recv()
-        hops[cc][3].start()
-        hops[cc][2].wait_recv()
-        hops[cc][4].start()
+    def arrive_then(cc, k, *forwards):
+        hops[cc][k].wait_recv()
+        for f in forwards:
+            hops[cc][f].start()
+
+    def forward_a(cc):
+        arrive_then(cc, 2, 6)
+        arrive_then(cc, 5, 7)
+        arrive_then(cc, 0, 8, 9)
+
+    def forward_b(cc):
+        arrive_then(cc, 1, 10, 11)
 
     def forward_two(cc):
-        hops[cc][3].wait_recv()
-        hops[cc][4].wait_recv()
-        hops[cc][7].start()
+        arrive_then(cc, 6, 12)
+        arrive_then(cc, 7, 13)
+
+    def near(cc):
+        arrive_then(cc, 3)
+        arrive_then(cc, 4)
 
     def finish(cc):
-        hops[cc][5].wait_recv()
-        hops[cc][6].wait_recv()
-        hops[cc][7].wait_recv()
+        for k in (8, 9, 10, 11, 12, 13):
+            arrive_then(cc, k)
         halos[cc].start()
 
     def halo(cc):
@@ -199,6 +219,7 @@
     halos = [halo(cc) for cc in range(CHUNKS)]
 
     sort_phases(0, 1)
+    pl.semaphore_wait(barrier, 22)
     own_sends(0)
     tab_cp = []
     for rel in range(1, 8):
@@ -209,6 +230,7 @@
         c.start()
         tab_cp.append(c)
     sort_phases(1, CHUNKS)
+    forward_a(0)
     tabs[u] = tab_ref[u]
     for c in tab_cp:
         c.wait_recv()
@@ -249,7 +271,7 @@
                 old_tall[at, :] = old_rows[:, src].astype(jnp.float32).T
                 return carry
 
-            lax.fori_loop(0, TAPS, turn, 0)
+            lax.fori_loop(0, TAPS, turn, 0, unroll=True)
             for j in range(STEP):
                 piece = old_tall[pl.ds(tg * STEP + j, WIDE, stride=TAPS), :].T
                 piece = jnp.where(tg * STEP + j < TAPS, piece, 0.0)
@@ -280,21 +302,29 @@
             swaps[cc - 1].wait_send()
         out = dot_f32(merge, snip[...].reshape(256, STEP * WIDE).astype(jnp.bfloat16))
         out = jnp.concatenate([out, tally], axis=1).reshape(4, 2, 2, 16, FLAT * WIDE)
-        sums[...] = out
-        away[...] = sums[:, :, 1 - core]
+        sums[cc] = out
+        away[...] = sums[cc, :, :, 1 - core]
         swaps[cc].start()
 
-    def y_send(cc, rel):
-        to = lax.rem(yy + rel, 4)
-        return remote(
-            part.at[cc, to],
-            part_in.at[cc, rel - 1],
-            ys_s.at[cc * 3 + rel - 1],
-            ys_r.at[cc * 3 + rel - 1],
-            {"tm": (to * 2 + xh) * 2 + core},
-        )
-
-    y_sends = [[y_send(cc, rel) for rel in (1, 2, 3)] for cc in range(CHUNKS)]
+    y_up, y_down, y_far = lax.rem(yy + 1, 4), lax.rem(yy + 3, 4), lax.rem(yy + 2, 4)
+    to_up = {"tm": (y_up * 2 + xh) * 2 + core}
+    to_down = {"tm": (y_down * 2 + xh) * 2 + core}
+
+    def y_plan(cc):
+        pairs = [
+            (part.at[cc, y_far, 0], via_in.at[cc, 0], to_up),
+            (part.at[cc, y_far, 1], via_in.at[cc, 1], to_down),
+            (part.at[cc, y_up], part_in.at[cc, 0], to_up),
+            (part.at[cc, y_down], part_in.at[cc, 1], to_down),
+            (via_in.at[cc, 0], far_in.at[cc, 0], to_up),
+            (via_in.at[cc, 1], far_in.at[cc, 1], to_down),
+        ]
+        return [
+            remote(src, dst, ys_s.at[cc * 6 + k], ys_r.at[cc * 6 + k], to)
+            for k, (src, dst, to) in enumerate(pairs)
+        ]
+
+    y_sends = [y_plan(cc) for cc in range(CHUNKS)]
     x_sends = [
         remote(side_out.at[cc], side_in.at[cc], xs_s.at[cc], xs_r.at[cc], {"tm": beside * 2 + core})
         for cc in range(CHUNKS)
@@ -302,23 +332,30 @@
 
     def reduce_one(cc):
         swaps[cc].wait_recv()
-        both = sums[:, :, core] + swap_in[cc]
+        both = sums[cc, :, :, core] + swap_in[cc]
         part[cc] = both.astype(jnp.bfloat16)
-        for c in y_sends[cc]:
+        for c in y_sends[cc][:4]:
             c.start()
-        sums[:, :, core] = both
+        sums[cc, :, :, core] = both
+
+    def relay_sums(cc):
+        for k in (0, 1):
+            y_sends[cc][k].wait_recv()
+            y_sends[cc][4 + k].start()
 
     def reduce_two(cc):
-        for c in y_sends[cc]:
+        for c in y_sends[cc][2:]:
             c.wait_recv()
-        far = sums[yy, 1 - xh, core]
-        near = sums[yy, xh, core]
-        for rel in range(3):
-            far = far + part_in[cc, rel, 1 - xh].astype(jnp.float32)
-            near = near + part_in[cc, rel, xh].astype(jnp.float32)
-        side_out[cc] = far.astype(jnp.bfloat16)
+
+        def total(x):
+            value = sums[cc, yy, x, core] + far_in[cc, x].astype(jnp.float32)
+            for k in (0, 1):
+                value = value + part_in[cc, k, x].astype(jnp.float32)
+            return value
+
+        side_out[cc] = total(1 - xh).astype(jnp.bfloat16)
         x_sends[cc].start()
-        keep[cc] = near
+        keep[cc] = total(xh)
 
     def panel(cc, ch, co):
         return t_ref.at[ch, co, :, cc * STEP * WIDE : (cc + 1) * STEP * WIDE]
@@ -327,16 +364,20 @@
         ref = panel(cc, chip, core)
         return remote(ref, ref, xg_s.at[cc], xg_r.at[cc], {"tm": beside * 2 + core})
 
-    def y_give(cc, rel, ch, k):
-        ref = panel(cc, ch, core)
-        to = lax.rem(yy + rel, 4)
-        return remote(
-            ref,
-            ref,
-            yg_s.at[cc * 6 + k * 3 + rel - 1],
-            yg_r.at[cc * 6 + k * 3 + rel - 1],
-            {"tm": (to * 2 + xh) * 2 + core},
-        )
+    def y_give_plan(cc):
+        pairs = [
+            (chip, to_up),
+            (chip, to_down),
+            (beside, to_up),
+            (beside, to_down),
+            (y_down * 2 + xh, to_up),
+            (y_up * 2 + 1 - xh, to_down),
+        ]
+        out = []
+        for k, (ch, to) in enumerate(pairs):
+            ref = panel(cc, ch, core)
+            out.append(remote(ref, ref, yg_s.at[cc * 6 + k], yg_r.at[cc * 6 + k], to))
+        return out
 
     def pass_on(cc, k, ch):
         ref = panel(cc, ch, core)
@@ -345,14 +386,17 @@
         )
 
     x_gives = [x_give(cc) for cc in range(CHUNKS)]
-    y_gives = [
-        [y_give(cc, rel, ch, k) for k, ch in ((0, chip), (1, beside)) for rel in (1, 2, 3)]
-        for cc in range(CHUNKS)
+    y_gives = [y_give_plan(cc) for cc in range(CHUNKS)]
+    origin = [
+        chip,
+        beside,
+        y_down * 2 + xh,
+        y_up * 2 + xh,
+        y_down * 2 + 1 - xh,
+        y_up * 2 + 1 - xh,
+        y_far * 2 + xh,
+        y_far * 2 + 1 - xh,
     ]
-    origin = [chip, beside]
-    for half_x in (xh, 1 - xh):
-        for rel in (1, 2, 3):
-            origin.append(lax.rem(yy + 4 - rel, 4) * 2 + half_x)
     passes = [[pass_on(cc, k, origin[k]) for k in range(8)] for cc in range(CHUNKS)]
 
     def refine(cc):
@@ -370,18 +414,25 @@
             fresh, axis=1
         ).astype(jnp.bfloat16)
         x_gives[cc].start()
-        for c in y_gives[cc][:3]:
+        for c in y_gives[cc][:2]:
             c.start()
         passes[cc][0].start()
 
     def spread_one(cc):
         x_gives[cc].wait_recv()
-        for c in y_gives[cc][3:]:
+        for c in y_gives[cc][2:4]:
             c.start()
         passes[cc][1].start()
 
     def spread_two(cc):
-        for k in range(6):
+        for k, then in ((0, 4), (3, 5), (1, None), (2, None)):
+            y_gives[cc][k].wait_recv()
+            if then is not None:
+                y_gives[cc][then].start()
+            passes[cc][2 + k].start()
+
+    def spread_three(cc):
+        for k in (4, 5):
             y_gives[cc][k].wait_recv()
             passes[cc][2 + k].start()
 
@@ -450,65 +501,73 @@
                     ]
         new_ref[...] = new_tall[...].T[0:64, 0 : 24 * TAPS].astype(jnp.bfloat16)
 
+    def gather_many(cc, positions):
+        for q in positions:
+            gather(cc, q)
+
+    forward_b(0)
+    own_sends(1)
     relay_old()
-
-    forward_one(0)
-    own_sends(1)
-    for q in range(4):
-        gather(0, q)
     forward_two(0)
+    near(0)
+    gather_many(0, (0, 1, 2, 3))
+    forward_a(1)
     gather(0, 4)
+    forward_b(1)
+    own_sends(2)
     finish(0)
-    for q in (5, 6, 7):
-        gather(0, q)
+    gather_many(0, (5, 6, 7))
     merge_labels(0)
 
-    forward_one(1)
-    own_sends(2)
+    forward_two(1)
+    near(1)
+    gather_many(1, (0, 1, 2))
     reduce_one(0)
-    for q in range(4):
-        gather(1, q)
-    forward_two(1)
-    gather(1, 4)
+    forward_a(2)
+    gather_many(1, (3, 4))
+    relay_sums(0)
+    forward_b(2)
+    finish(1)
+    forward_two(2)
+    gather_many(1, (5, 6, 7))
+    merge_labels(1)
     reduce_two(0)
-    finish(1)
+
+    near(2)
+    gather_many(2, (0, 1, 2))
+    reduce_one(1)
     refine(0)
-    for q in (5, 6, 7):
-        gather(1, q)
-    merge_labels(1)
-
-    forward_one(2)
+    gather_many(2, (3, 4))
+    relay_sums(1)
     spread_one(0)
-    reduce_one(1)
-    for q in range(4):
-        gather(2, q)
-    forward_two(2)
-    gather(2, 4)
+    finish(2)
+    gather_many(2, (5, 6, 7))
+    merge_labels(2)
+
+    spread_two(0)
     reduce_two(1)
-    spread_two(0)
-    finish(2)
+    reduce_one(2)
+    spread_three(0)
     refine(1)
-    for q in (5, 6, 7):
-        gather(2, q)
-    merge_labels(2)
-
-    spread_one(1)
+    relay_sums(2)
     settle(0)
     correlate(0, 0)
-    reduce_one(2)
+    spread_one(1)
     correlate(0, 1)
     spread_two(1)
+    reduce_two(2)
     correlate(0, 2)
+    spread_three(1)
     correlate(0, 3)
-    reduce_two(2)
+    refine(2)
     settle(1)
     correlate(1, 0)
-    refine(2)
     correlate(1, 1)
     spread_one(2)
     correlate(1, 2)
+    spread_two(2)
     correlate(1, 3)
-    spread_two(2)
+    spread_three(2)
     settle(2)
     for d in range(4):
         correlate(2, d)
@@ -548,11 +607,13 @@
             pltpu.VMEM((8, CAP, 128), jnp.int32),
             pltpu.VMEM((8, GROUPS * STEP * CAP, 1024), bf16),
             pltpu.VMEM((GROUPS, 64, STEP * WIDE), f32),
-            pltpu.VMEM((4, 2, 2, 16, flat), f32),
+            pltpu.VMEM((CHUNKS, 4, 2, 2, 16, flat), f32),
             pltpu.VMEM((4, 2, 16, flat), f32),
             pltpu.VMEM((CHUNKS, 4, 2, 16, flat), f32),
             pltpu.VMEM((CHUNKS, 4, 2, 16, flat), bf16),
-            pltpu.VMEM((CHUNKS, 3, 2, 16, flat), bf16),
+            pltpu.VMEM((CHUNKS, 2, 2, 16, flat), bf16),
+            pltpu.VMEM((CHUNKS, 2, 16, flat), bf16),
+            pltpu.VMEM((CHUNKS, 2, 16, flat), bf16),
             pltpu.VMEM((CHUNKS, 16, flat), f32),
             pltpu.VMEM((CHUNKS, 16, flat), bf16),
             pltpu.VMEM((CHUNKS, 16, flat), bf16),
@@ -562,14 +623,14 @@
             dma,
             dma((7,)),
             dma((7,)),
-            dma((CHUNKS * 8,)),
-            dma((CHUNKS * 8,)),
-            dma((CHUNKS,)),
-            dma((CHUNKS,)),
-            dma((CHUNKS,)),
-            dma((CHUNKS,)),
-            dma((CHUNKS * 3,)),
-            dma((CHUNKS * 3,)),
+            dma((CHUNKS * 14,)),
+            dma((CHUNKS * 14,)),
+            dma((CHUNKS,)),
+            dma((CHUNKS,)),
+            dma((CHUNKS,)),
+            dma((CHUNKS,)),
+            dma((CHUNKS * 6,)),
+            dma((CHUNKS * 6,)),
             dma((CHUNKS,)),
             dma((CHUNKS,)),
             dma((CHUNKS,)),

time: 145 us -> 114 us (0.79)
  Pallas kernels: 138 us -> 108 us
    pallas_call x1, Pallas kernels: 138 us -> 108 us  [refine_and_correlate(): pl.pallas_call(functools.partial(refine_kernel, scale), out_shape=(jax.Sh...]
where the time goes in v3:
time: 114 us
  Pallas kernels  108 us (95%)
  local copies, waits for them, and re-layouts  4.04 us (4%)
  other arithmetic  1.69 us (1%)
    pallas_call x1, Pallas kernels, refine_and_correlate(): pl.pallas_call(functools.partial(refine_kernel, scale), out_shape=(jax.Sh...  108 us
    unnamed x2, local copies, waits for them, and re-layouts  3.89 us

profile of v3, /device:TPU:1, one launch (start us, length us, event | category | flops | bytes accessed | tf_op | source)
XLA Modules:
  0.0 113.9 jit_solution(10898195056792457417)
XLA Ops:
  0.6 0.7 fusion.1
  1.3 0.2 convert_reduce_fusion
  1.5 0.1 select_reduce_fusion.1
  1.6 0.1 sub.27
  1.7 0.1 broadcast_in_dim.58
  1.8 0.7 broadcast_select_fusion.tab_ref
  2.5 107.6 %refine_and_correlate.1 = (bf16[64,1464]{1,0:T(8,128)(2,1)}, f32[64,4096]{1,0:T(8,128)}) custom-call(bf16[1024,384]{1,0:T(8,128)(2,1)} %own_ref.1, s32[8,8,128]{2,1,0:T(8,128)} %broadcast_select_fusion.tab_ref, bf16[64,23424]{1,0:T(8,128)(2,1)} %old_ref.1), custom_call_target="tpu_custom_call" | custom-call | tf_op jit(solution)/shard_map/refine_and_correlate/pallas_call | solution.py:593
  110.1 1.6 %copy.8 = bf16[64,1464]{1,0:T(8,128)(2,1)} copy(bf16[64,1464]{1,0:T(8,128)(2,1)} %get-tuple-element.9) | data formatting | bytes 374784
  111.7 2.3 %copy.9 = f32[64,4096]{1,0:T(8,128)} copy(f32[64,4096]{1,0:T(8,128)} %get-tuple-element.10) | data formatting | bytes 2097152
  (3 shorter events, 0.0 us)

commit v4 on v3

--- a/solution.py
+++ b/solution.py
@@ -19,7 +19,7 @@
 CHUNKS = 3
 WIDE = 128
 FLAT = STEP + 1
-SIZE = ROWS // 2
+SIZE = 1040
 LONG = TAPS * WIDE
 
 
@@ -37,10 +37,13 @@
 def refine_kernel(
     scale,
     own_ref,
-    tab_ref,
+    times_ref,
+    labels_ref,
     old_ref,
     new_ref,
     score_ref,
+    plain,
+    tab_ref,
     x_ref,
     t_ref,
     old_rows,
@@ -113,20 +116,34 @@
         pl.semaphore_signal(
             barrier, inc=1, device_id={"tm": lax.rem(t + rel, 16)}, device_id_type=MESH
         )
-    row = lax.broadcasted_iota(jnp.int32, (LINES, 1024), 0) * PHASES
-    col = lax.broadcasted_iota(jnp.int32, (LINES, 1024), 1)
     mine = pl.ds(pl.multiple_of(u * LINES, LINES), LINES)
 
-    def sort_phases(first, last):
-        own = own_ref[:, first * WIDE : last * WIDE]
+    def sort_phases(cc):
+        plain[...] = own_ref[:, cc * WIDE : (cc + 1) * WIDE].astype(jnp.float32)
         for p in range(PHASES):
-            pick = jnp.where(col == row + p, 1.0, 0.0).astype(jnp.bfloat16)
-            got = dot_f32(pick, own).astype(jnp.bfloat16)
-            for cc in range(first, last):
-                lane = (cc * PHASES + p) * WIDE
-                x_ref[mine, lane : lane + WIDE] = got[
-                    :, (cc - first) * WIDE : (cc - first + 1) * WIDE
-                ]
+            lane = (cc * PHASES + p) * WIDE
+            got = plain[pl.ds(p, LINES, stride=PHASES), :]
+            x_ref[mine, lane : lane + WIDE] = got.astype(jnp.bfloat16)
+
+    def build_table():
+        f32 = jnp.float32
+        labels = labels_ref[...]
+        start = (times_ref[...] - (t * 8 + u) * 1024 - (TAPS - 1) // 2).astype(f32)
+        owner = lax.shift_right_logical(labels, 6).astype(f32)
+        within = jnp.bitwise_and(labels, 63).astype(f32)
+        spikes = labels.shape[1]
+        i0 = lax.broadcasted_iota(jnp.int32, (spikes, spikes), 0)
+        i1 = lax.broadcasted_iota(jnp.int32, (spikes, spikes), 1)
+        owner_tall = jnp.sum(jnp.where(i0 == i1, owner, 0.0), axis=1, keepdims=True)
+        ahead = jnp.logical_and(owner_tall == owner, i0 < i1)
+        rank = jnp.sum(jnp.where(ahead, 1.0, 0.0), axis=0, keepdims=True)
+        slot = owner * CAP + rank
+        place = lax.broadcasted_iota(jnp.int32, (8 * CAP, spikes), 0).astype(f32)
+        hit = place == slot
+        start_of = jnp.sum(jnp.where(hit, start, 0.0), axis=1, keepdims=True)
+        label_of = jnp.sum(jnp.where(hit, within + 1.0, 0.0), axis=1, keepdims=True) - 1.0
+        lane = lax.broadcasted_iota(jnp.int32, (8 * CAP, 128), 1)
+        tab_ref[...] = jnp.where(lane < 64, start_of, label_of).reshape(8, CAP, 128)
 
     def block(index, cc, first=0, count=LINES):
         return x_ref.at[
@@ -218,9 +235,10 @@
 
     halos = [halo(cc) for cc in range(CHUNKS)]
 
-    sort_phases(0, 1)
+    sort_phases(0)
     pl.semaphore_wait(barrier, 22)
     own_sends(0)
+    build_table()
     tab_cp = []
     for rel in range(1, 8):
         to = lax.rem(u + rel, 8)
@@ -229,17 +247,18 @@
         )
         c.start()
         tab_cp.append(c)
-    sort_phases(1, CHUNKS)
+    sort_phases(1)
+    sort_phases(2)
     forward_a(0)
     tabs[u] = tab_ref[u]
     for c in tab_cp:
         c.wait_recv()
 
     tval = lax.broadcasted_iota(jnp.int32, (CAP, 1024), 1)
-    tval = (tval % LINES) * PHASES + tval // LINES
+    tval = ((tval % LINES) * PHASES + tval // LINES).astype(jnp.float32)
     lead = lax.broadcasted_iota(jnp.int32, (GROUPS * STEP, 1, 1), 0)
     tap = (lead % GROUPS) * STEP + lead // GROUPS
-    tap = jnp.where(tap < TAPS, tap, -100000)
+    tap = jnp.where(tap < TAPS, tap, -100000).astype(jnp.float32)
     order = [u, across, up, down, side + zo, other + zp, other + zm, other + zo]
 
     def build_picks(i, carry):
@@ -255,8 +274,9 @@
     labels = jnp.concatenate([labels] * GROUPS, axis=0)
     r4 = lax.broadcasted_iota(jnp.int32, (256, 256), 0)
     c4 = lax.broadcasted_iota(jnp.int32, (256, 256), 1)
+    unit_of = (c4 % 64).astype(jnp.float32)
     merge = jnp.where(
-        jnp.logical_and(labels == c4 % 64, r4 // 64 == c4 // 64), 1.0, 0.0
+        jnp.logical_and(labels == unit_of, r4 // 64 == c4 // 64), 1.0, 0.0
     )
     merge = merge.T.astype(jnp.bfloat16)
     tally = dot_f32(merge, jnp.ones((256, WIDE), jnp.bfloat16))
@@ -449,7 +469,7 @@
 
     def correlate(cc, d):
         def one(i, carry):
-            first = pl.multiple_of(i * SIZE, 16)
+            first = 0
             for at, (dd, e) in enumerate(PLANES):
                 if dd != d:
                     continue
@@ -466,7 +486,7 @@
                     y_ref[at, pl.ds(first, SIZE), :] += total
             return carry
 
-        lax.fori_loop(0, 2, one, 0)
+        one(0, 0)
 
     def collect(d):
         a = None
@@ -548,22 +568,22 @@
     reduce_two(1)
     reduce_one(2)
     spread_three(0)
+    relay_sums(2)
     refine(1)
-    relay_sums(2)
     settle(0)
     correlate(0, 0)
+    correlate(0, 1)
     spread_one(1)
-    correlate(0, 1)
-    spread_two(1)
     reduce_two(2)
     correlate(0, 2)
-    spread_three(1)
+    spread_two(1)
     correlate(0, 3)
     refine(2)
+    spread_three(1)
     settle(1)
     correlate(1, 0)
+    spread_one(2)
     correlate(1, 1)
-    spread_one(2)
     correlate(1, 2)
     spread_two(2)
     correlate(1, 3)
@@ -585,7 +605,7 @@
             c.wait_send()
 
 
-def refine_and_correlate(own, tab, old, scale):
+def refine_and_correlate(own, times, labels, old, scale):
     bf16, f32 = jnp.bfloat16, jnp.float32
     dma = pltpu.SemaphoreType.DMA
     vmem = pl.BlockSpec(memory_space=pltpu.VMEM)
@@ -596,15 +616,17 @@
             jax.ShapeDtypeStruct((64, 24 * TAPS), bf16),
             jax.ShapeDtypeStruct((64, 4096), f32),
         ),
-        in_specs=[vmem, vmem, pl.BlockSpec(memory_space=pl.ANY)],
+        in_specs=[vmem, vmem, vmem, pl.BlockSpec(memory_space=pl.ANY)],
         out_specs=[vmem] * 2,
         scratch_shapes=[
+            pltpu.VMEM((1024, WIDE), f32),
+            pltpu.VMEM((8, CAP, 128), f32),
             pltpu.VMEM((ROWS, CHUNKS * PHASES * WIDE), bf16),
             pltpu.VMEM((8, 2, 16, CHUNKS * STEP * WIDE), bf16),
             pltpu.VMEM((16, CHUNKS * LONG), bf16),
             pltpu.VMEM((LONG + 64, 16), f32),
             pltpu.VMEM((CHUNKS, 16, STEP * WIDE), f32),
-            pltpu.VMEM((8, CAP, 128), jnp.int32),
+            pltpu.VMEM((8, CAP, 128), f32),
             pltpu.VMEM((8, GROUPS * STEP * CAP, 1024), bf16),
             pltpu.VMEM((GROUPS, 64, STEP * WIDE), f32),
             pltpu.VMEM((CHUNKS, 4, 2, 2, 16, flat), f32),
@@ -644,30 +666,14 @@
             collective_id=0, has_side_effects=True, vmem_limit_bytes=62 << 20
         ),
         name="refine_and_correlate",
-    )(own, tab, old)
+    )(own, times, labels, old)
 
 
 def body(recording, spike_times, unit_labels, old_templates):
-    sub_rows = recording.shape[0]
-    panel, feat = old_templates.shape
-    spikes = spike_times.shape[0]
-    t = lax.axis_index("tm")
-    u = lax.axis_index("unit")
-    start = spike_times - (t * 8 + u) * sub_rows - (TAPS - 1) // 2
-    owner = unit_labels // panel
-    within = unit_labels % panel
-    before = jnp.arange(spikes)[None, :] < jnp.arange(spikes)[:, None]
-    rank = jnp.sum(
-        jnp.logical_and(owner[:, None] == owner[None, :], before).astype(jnp.int32), axis=1
-    )
-    slot = owner * CAP + rank
-    hit = jnp.arange(8 * CAP)[:, None] == slot[None, :]
-    start_of = jnp.sum(jnp.where(hit, start[None, :], 0), axis=1)
-    label_of = jnp.sum(jnp.where(hit, within[None, :] + 1, 0), axis=1) - 1
-    lane = jnp.arange(128)[None, :]
-    tab = jnp.where(lane < 64, start_of[:, None], label_of[:, None]).reshape(8, CAP, 128)
-    scale = 1.0 / (feat**0.5)
-    return refine_and_correlate(recording, tab.astype(jnp.int32), old_templates, scale)
+    feat = old_templates.shape[1]
+    times = spike_times.reshape(1, -1)
+    labels = unit_labels.reshape(1, -1)
+    return refine_and_correlate(recording, times, labels, old_templates, 1.0 / (feat**0.5))
 
 
 def solution(mesh):

time: 114 us -> 108 us (0.947)
  Pallas kernels: 108 us -> 104 us
  other arithmetic: 1.69 us -> 0 us
    pallas_call x1, Pallas kernels: 108 us -> 104 us  [refine_and_correlate(): pl.pallas_call(functools.partial(refine_kernel, scale), out_shape=(jax.Sh...]
where the time goes in v4:
time: 108 us
  Pallas kernels  104 us (96%)
  local copies, waits for them, and re-layouts  3.89 us (4%)
    pallas_call x1, Pallas kernels, refine_and_correlate(): pl.pallas_call(functools.partial(refine_kernel, scale), out_shape=(jax.Sh...  104 us
    unnamed x2, local copies, waits for them, and re-layouts  3.89 us

profile of v4, /device:TPU:1, one launch (start us, length us, event | category | flops | bytes accessed | tf_op | source)
XLA Modules:
  0.0 108.3 jit_solution(3084805839807273331)
XLA Ops:
  0.6 103.8 %refine_and_correlate.1 = (bf16[64,1464]{1,0:T(8,128)(2,1)}, f32[64,4096]{1,0:T(8,128)}) custom-call(bf16[1024,384]{1,0:T(8,128)(2,1)} %own_ref.1, s32[1,32]{1,0:T(1,128)} %bitcast.2, s32[1,32]{1,0:T(1,128)} %bitcast.3, bf16[64,23424]{1,0:T(8,128)(2,1)} %old_ref.1), custom_call_target="tpu_custom_call" | custom-call | tf_op jit(solution)/shard_map/refine_and_correlate/pallas_call | solution.py:613
  104.4 1.6 %copy.8 = bf16[64,1464]{1,0:T(8,128)(2,1)} copy(bf16[64,1464]{1,0:T(8,128)(2,1)} %get-tuple-element.4) | data formatting | bytes 374784
  106.0 2.3 %copy.9 = f32[64,4096]{1,0:T(8,128)} copy(f32[64,4096]{1,0:T(8,128)} %get-tuple-element.5) | data formatting | bytes 2097152

commit v5 on v4

--- a/solution.py
+++ b/solution.py
@@ -250,6 +250,7 @@
     sort_phases(1)
     sort_phases(2)
     forward_a(0)
+    own_sends(1)
     tabs[u] = tab_ref[u]
     for c in tab_cp:
         c.wait_recv()
@@ -526,15 +527,14 @@
             gather(cc, q)
 
     forward_b(0)
-    own_sends(1)
     relay_old()
     forward_two(0)
     near(0)
     gather_many(0, (0, 1, 2, 3))
     forward_a(1)
+    own_sends(2)
     gather(0, 4)
     forward_b(1)
-    own_sends(2)
     finish(0)
     gather_many(0, (5, 6, 7))
     merge_labels(0)

time: 108 us -> 109 us (level)
  no operation moved by 1% of the time
where the time goes in v5:
time: 109 us; the launch traced here: 108 us
  Pallas kernels  104 us (95%)
  local copies, waits for them, and re-layouts  3.89 us (4%)
    pallas_call x1, Pallas kernels, refine_and_correlate(): pl.pallas_call(functools.partial(refine_kernel, scale), out_shape=(jax.Sh...  104 us
    unnamed x2, local copies, waits for them, and re-layouts  3.89 us

profile of v5, /device:TPU:1, one launch (start us, length us, event | category | flops | bytes accessed | tf_op | source)
XLA Modules:
  0.0 108.4 jit_solution(12158576808274659417)
XLA Ops:
  0.6 103.9 %refine_and_correlate.1 = (bf16[64,1464]{1,0:T(8,128)(2,1)}, f32[64,4096]{1,0:T(8,128)}) custom-call(bf16[1024,384]{1,0:T(8,128)(2,1)} %own_ref.1, s32[1,32]{1,0:T(1,128)} %bitcast.2, s32[1,32]{1,0:T(1,128)} %bitcast.3, bf16[64,23424]{1,0:T(8,128)(2,1)} %old_ref.1), custom_call_target="tpu_custom_call" | custom-call | tf_op jit(solution)/shard_map/refine_and_correlate/pallas_call | solution.py:613
  104.6 1.6 %copy.8 = bf16[64,1464]{1,0:T(8,128)(2,1)} copy(bf16[64,1464]{1,0:T(8,128)(2,1)} %get-tuple-element.4) | data formatting | bytes 374784
  106.2 2.3 %copy.9 = f32[64,4096]{1,0:T(8,128)} copy(f32[64,4096]{1,0:T(8,128)} %get-tuple-element.5) | data formatting | bytes 2097152
